TPU v7x, 512 devices: a whole 4x8x8 slice. The times are simulated.
512 devices in a mesh: grp: 8 (over x, core), blk: 64 (over y, z).
Axes of the slice: x: 4, y: 8, z: 8, core: 2. Of those that a mesh axis runs over, the one named last changes fastest.
Arguments:
- features: bfloat16 [65536, 256], P(('grp', 'blk')), may hold values from -6 to 6
- dest: int32 [65536, 1], P(('grp', 'blk')), may hold values from 0 to 63; in each aligned block of 128 rows (0 to 127, 128 to 255, ...) at most 4 rows name the same one
- placement: int32 [512, 256], P(('grp', 'blk')), may hold values from 0 to 255, each once within a row
- weight: bfloat16 [27, 256, 128], replicated, may hold values from -0.078125 to 0.078125
- grad_out: bfloat16 [64, 512, 4, 128], P('grp', 'blk'), may hold values from -6 to 6
Outputs:
- output: bfloat16 [64, 512, 4, 128], P('grp', 'blk')
- grad_rows: bfloat16 [65536, 256], P(('grp', 'blk'))
- weight_grad: bfloat16 [27, 256, 128], replicated
Inputs may be any that keep to these rules, and one draw needn't show every extreme that they name: `dest`: among the rows of one device no value is named by more than 4 rows, a bound that some block reaches. `placement`: each row is a permutation of 0 to 255.
All inputs are finite; a program needn't handle non-finite values.
Results may differ from a plain program's by a relative error of at most 0.0013.
Values may be sent and summed in bfloat16 or wider, within the bound.
A program may use at most 64 MiB of HBM per device.

v0:
```python
import math

import jax
import jax.numpy as jnp
from jax import lax
from jax.sharding import PartitionSpec as P


def extended(cells, sides, width):
    for axis, dim in sides:
        count = lax.axis_size(axis)
        ends = count - 1
        head = lax.slice_in_dim(cells, 0, width, axis=dim)
        tail = lax.slice_in_dim(cells, cells.shape[dim] - width, cells.shape[dim], axis=dim)
        cells = jnp.concatenate(
            [
                lax.ppermute(tail, axis, [(i, (i + 1) % count) for i in range(ends)]),
                cells,
                lax.ppermute(head, axis, [((i + 1) % count, i) for i in range(ends)]),
            ],
            axis=dim,
        )
    return cells


def shards(features, dest, placement, weight, grad_out):
    row_count, channels = features.shape
    blk_count = lax.axis_size("blk")
    grp_count = lax.axis_size("grp")
    voxel_of_slot = placement[0]
    voxel_count = voxel_of_slot.shape[0]
    capacity = voxel_count // blk_count
    size_x, size_y, size_z, out_channels = grad_out.shape
    target = dest[:, 0]
    owners = jnp.arange(blk_count, dtype=jnp.int32)
    one_hot = (target[:, None] == owners[None, :]).astype(jnp.int32)
    slot_rank = jnp.sum((jnp.cumsum(one_hot, axis=0) - one_hot) * one_hot, axis=1)
    send_counts = jnp.sum(one_hot, axis=0).reshape(blk_count, 1)
    slot_index = target * capacity + slot_rank
    outgoing = jnp.zeros((voxel_count, channels), jnp.bfloat16).at[slot_index].set(features)
    incoming, recv_counts = (
        lax.all_to_all(
            outgoing.reshape(blk_count, capacity, channels),
            "blk",
            split_axis=0,
            concat_axis=0,
            tiled=True,
        ),
        lax.all_to_all(send_counts, "blk", split_axis=0, concat_axis=0, tiled=True),
    )
    filled = (
        (jnp.arange(capacity, dtype=jnp.int32)[None, :] < recv_counts)
        .reshape(-1)
        .astype(jnp.float32)
    )
    voxel_rows = (
        jnp.zeros((voxel_count, channels), jnp.bfloat16)
        .at[voxel_of_slot]
        .set(incoming.reshape(voxel_count, channels))
    )
    occupied = jnp.zeros((voxel_count,), jnp.float32).at[voxel_of_slot].set(filled)[:, None]
    voxel_grid = voxel_rows.reshape(size_x, size_y, size_z, channels)
    padded = extended(voxel_grid, (("grp", 0), ("blk", 1)), 1)
    padded = jnp.pad(padded, ((0, 0), (0, 0), (1, 1), (0, 0)))
    shifted = []
    total = jnp.zeros((voxel_count, out_channels), jnp.float32)
    for offset in range(27):
        shift_x, shift_y, shift_z = (offset // 9, offset // 3 % 3, offset % 3)
        window = padded[
            shift_x : shift_x + size_x, shift_y : shift_y + size_y, shift_z : shift_z + size_z
        ].reshape(voxel_count, channels)
        shifted.append(window)
        total = total + jnp.dot(window, weight[offset], preferred_element_type=jnp.float32)
    output = (total * occupied).astype(jnp.bfloat16).reshape(size_x, size_y, size_z, out_channels)
    masked_grad = (
        grad_out.reshape(voxel_count, out_channels).astype(jnp.float32) * occupied
    ).astype(jnp.bfloat16)
    grad_padded = extended(
        masked_grad.reshape(size_x, size_y, size_z, out_channels), (("grp", 0), ("blk", 1)), 1
    )
    grad_padded = jnp.pad(grad_padded, ((0, 0), (0, 0), (1, 1), (0, 0)))
    back_total = jnp.zeros((voxel_count, channels), jnp.float32)
    partials = []
    for offset in range(27):
        shift_x, shift_y, shift_z = (offset // 9, offset // 3 % 3, offset % 3)
        window = grad_padded[
            2 - shift_x : 2 - shift_x + size_x,
            2 - shift_y : 2 - shift_y + size_y,
            2 - shift_z : 2 - shift_z + size_z,
        ].reshape(voxel_count, out_channels)
        back_total = back_total + lax.dot_general(
            window, weight[offset], (((1,), (1,)), ((), ())), preferred_element_type=jnp.float32
        )
        partials.append(
            lax.dot_general(
                shifted[offset],
                masked_grad,
                (((0,), (0,)), ((), ())),
                preferred_element_type=jnp.float32,
            )
        )
    grad_grid = (back_total * occupied).astype(jnp.bfloat16)
    weight_terms = jnp.stack(partials).reshape(27 * channels, out_channels)
    grad_scale = 1.0 / math.sqrt(row_count * blk_count * grp_count)
    weight_grad = (lax.psum(weight_terms, ("grp", "blk")) * grad_scale).astype(jnp.bfloat16)
    weight_grad = weight_grad.reshape(27, channels, out_channels)
    returning = grad_grid[voxel_of_slot].reshape(blk_count, capacity, channels)
    returned = lax.all_to_all(returning, "blk", split_axis=0, concat_axis=0, tiled=True)
    grad_rows = returned.reshape(voxel_count, channels)[slot_index]
    return (output, grad_rows, weight_grad)


def solution(mesh):
    in_specs = (
        P(("grp", "blk"), None),
        P(("grp", "blk"), None),
        P(("grp", "blk"), None),
        P(),
        P("grp", "blk", None, None),
    )
    out_specs = (P("grp", "blk", None, None), P(("grp", "blk"), None), P())
    return jax.shard_map(shards, mesh=mesh, in_specs=in_specs, out_specs=out_specs, check_vma=False)
```

profile of v0, /device:TPU:1, one launch (start us, length us, event | category | flops | bytes accessed | tf_op | source)
XLA Modules:
  0.0 479.5 jit_solution(8768574311076272875)
XLA Ops:
  9.6 17.1 %all-to-all-start.1 = ((s32[64,1,1]{2,1,0:T(1,128)}), s32[64,1,1]{2,1,0:T(1,128)S(1)}, u32[]{:S(2)}, u32[]{:S(2)}) async-start(s32[64,1,1]{2,1,0:T(1,128)} %copy.183), calls=%async_computation.1 | async-start | bytes 65536 | tf_op jit(solution)/shard_map/all_to_all | solution.py:49
  30.2 7.3 %all-to-all-done.1 = s32[64,1,1]{2,1,0:T(1,128)S(1)} async-done(((s32[64,1,1]{2,1,0:T(1,128)}), s32[64,1,1]{2,1,0:T(1,128)S(1)}, u32[]{:S(2)}, u32[]{:S(2)}) %all-to-all-start.1) | async-done | bytes 288 | tf_op jit(solution)/shard_map/all_to_all | solution.py:49
  37.5 4.8 %all-to-all-start = ((bf16[64,4,256]{2,1,0:T(4,128)(2,1)}), bf16[64,4,256]{2,1,0:T(4,128)(2,1)S(1)}, u32[]{:S(2)}, u32[]{:S(2)}) async-start(bf16[64,4,256]{2,1,0:T(4,128)(2,1)} %reshape.379), calls=%async_computation | async-start | bytes 262144 | tf_op jit(solution)/shard_map/all_to_all | solution.py:42
  46.3 3.8 collective-permute-start.5
  50.1 3.0 collective-permute-start.4
  54.1 3.1 collective-permute-start.6
  58.6 3.0 collective-permute-done.7
  69.1 5.4 %collective-permute-start = (bf16[1,8,4,256]{3,1,2,0:T(8,128)(2,1)S(1)}, bf16[1,8,4,256]{3,1,2,0:T(8,128)(2,1)S(1)}, u32[]{:S(2)}, u32[]{:S(2)}) collective-permute-start(bf16[1,8,4,256]{3,1,2,0:T(8,128)(2,1)S(1)} %copy.152), channel_id=1, source_target_pairs={{0,64},{64,128},{128,192},{192,256},{256,320},{320,384},{384,448},... | collective-permute-start | bytes 49160 | tf_op jit(solution)/shard_map/ppermute | solution.py:17
  76.5 12.7 %all-to-all-start.2 = ((bf16[64,4,256]{2,1,0:T(4,128)(2,1)}), bf16[64,4,256]{2,1,0:T(4,128)(2,1)S(1)}, u32[]{:S(2)}, u32[]{:S(2)}) async-start(bf16[64,4,256]{2,1,0:T(4,128)(2,1)} %reshape.436), calls=%async_computation.2 | async-start | bytes 262144 | tf_op jit(solution)/shard_map/all_to_all | solution.py:108
  89.4 1.9 collective-permute-start.1
  91.4 3.3 collective-permute-done.1
  94.8 2.9 collective-permute-start.2
  120.3 1.6 copy.176
  123.5 1.6 copy.175
  126.7 1.6 copy.173
  129.9 1.6 copy.172
  133.1 1.6 copy.170
  134.7 1.6 reshape.396
  149.1 1.6 copy.164
  152.3 1.6 copy.162
  156.2 1.6 reshape.387
  184.0 1.8 copy-done.2
  189.9 279.4 %all-reduce.4.cloned.1.call-done = f32[6912,128]{1,0:T(8,128)} async-done(((f32[6912,128]{1,0:T(8,128)}), f32[6912,128]{1,0:T(8,128)}) %all-reduce.4.cloned.1.call-update) | async-done | bytes 3538960 | tf_op jit(solution)/shard_map/psum | solution.py:105
  469.3 3.4 multiply_convert_fusion
  (246 shorter events, 96.7 us)
Async XLA Ops:
  9.6 27.9 %all-to-all-start.1 = ((s32[64,1,1]{2,1,0:T(1,128)}), s32[64,1,1]{2,1,0:T(1,128)S(1)}, u32[]{:S(2)}, u32[]{:S(2)}) async-start(s32[64,1,1]{2,1,0:T(1,128)} %copy.183), calls=%async_computation.1 | async-start | bytes 65536 | tf_op jit(solution)/shard_map/all_to_all | solution.py:49
  37.5 30.0 %all-to-all-start = ((bf16[64,4,256]{2,1,0:T(4,128)(2,1)}), bf16[64,4,256]{2,1,0:T(4,128)(2,1)S(1)}, u32[]{:S(2)}, u32[]{:S(2)}) async-start(bf16[64,4,256]{2,1,0:T(4,128)(2,1)} %reshape.379), calls=%async_computation | async-start | bytes 262144 | tf_op jit(solution)/shard_map/all_to_all | solution.py:42
  42.4 19.8 %copy-start = (bf16[27,256,128]{2,1,0:T(8,128)(2,1)S(1)}, bf16[27,256,128]{2,1,0:T(8,128)(2,1)}, u32[]{:S(2)}) copy-start(bf16[27,256,128]{2,1,0:T(8,128)(2,1)} %param.8) | copy-start | bytes 5308420
  46.3 7.8 %collective-permute-start.5 = (bf16[1,8,4,128]{3,2,1,0:T(4,128)(2,1)S(1)}, bf16[1,8,4,128]{3,2,1,0:T(4,128)(2,1)S(1)}, u32[]{:S(2)}, u32[]{:S(2)}) collective-permute-start(bf16[1,8,4,128]{3,2,1,0:T(4,128)(2,1)S(1)} %bitcast.495), channel_id=1, source_target_pairs={{64,0},{128,64},{192,128},{256,192},{320,256},{384,320},{448,384},... | collective-permute-start | bytes 24584 | tf_op jit(solution)/shard_map/ppermute | solution.py:19
  50.1 4.0 collective-permute-start.4
  54.1 4.5 collective-permute-start.6
  57.2 4.4 collective-permute-start.7
  69.1 22.2 %collective-permute-start = (bf16[1,8,4,256]{3,1,2,0:T(8,128)(2,1)S(1)}, bf16[1,8,4,256]{3,1,2,0:T(8,128)(2,1)S(1)}, u32[]{:S(2)}, u32[]{:S(2)}) collective-permute-start(bf16[1,8,4,256]{3,1,2,0:T(8,128)(2,1)S(1)} %copy.152), channel_id=1, source_target_pairs={{0,64},{64,128},{128,192},{192,256},{256,320},{320,384},{384,448},... | collective-permute-start | bytes 49160 | tf_op jit(solution)/shard_map/ppermute | solution.py:17
  76.5 24.2 %all-to-all-start.2 = ((bf16[64,4,256]{2,1,0:T(4,128)(2,1)}), bf16[64,4,256]{2,1,0:T(4,128)(2,1)S(1)}, u32[]{:S(2)}, u32[]{:S(2)}) async-start(bf16[64,4,256]{2,1,0:T(4,128)(2,1)} %reshape.436), calls=%async_computation.2 | async-start | bytes 262144 | tf_op jit(solution)/shard_map/all_to_all | solution.py:108
  89.2 380.0 %all-reduce.4.cloned.1.call-start = ((), (), s32[]{:S(2)}) async-start(), calls=%async_computation.3 | async-start | bytes 7077888 | tf_op jit(solution)/shard_map/psum | solution.py:105
  89.3 9.9 %copy-start.18 = (bf16[8,8,4,256]{3,2,1,0:T(4,128)(2,1)}, bf16[8,8,4,256]{3,2,1,0:T(4,128)(2,1)S(1)}, u32[]{:S(2)}) copy-start(bf16[8,8,4,256]{3,2,1,0:T(4,128)(2,1)S(1)} %reshape.381) | copy-start | bytes 393220
  89.4 5.4 %collective-permute-start.1 = (bf16[1,8,4,256]{3,1,2,0:T(8,128)(2,1)S(1)}, bf16[1,8,4,256]{3,1,2,0:T(8,128)(2,1)S(1)}, u32[]{:S(2)}, u32[]{:S(2)}) collective-permute-start(bf16[1,8,4,256]{3,1,2,0:T(8,128)(2,1)S(1)} %copy.153), channel_id=1, source_target_pairs={{64,0},{128,64},{192,128},{256,192},{320,256},{384,320},{448,384},... | collective-permute-start | bytes 49160 | tf_op jit(solution)/shard_map/ppermute | solution.py:19
  91.4 10.9 %copy-start.31 = (bf16[9,8,4,256]{3,1,2,0:T(8,128)(2,1)}, bf16[9,8,4,256]{3,1,2,0:T(8,128)(2,1)S(1)}, u32[]{:S(2)}) copy-start(bf16[9,8,4,256]{3,1,2,0:T(8,128)(2,1)S(1)} %get-tuple-element.53) | copy-start | bytes 442372
  94.7 4.5 copy-start.27
  94.8 7.5 %collective-permute-start.2 = (bf16[10,1,4,256]{3,1,2,0:T(2,128)(2,1)S(1)}, bf16[10,1,4,256]{3,1,2,0:T(2,128)(2,1)S(1)}, u32[]{:S(2)}, u32[]{:S(2)}) collective-permute-start(bf16[10,1,4,256]{3,1,2,0:T(2,128)(2,1)S(1)} %get-tuple-element.50), channel_id=1, source_target_pairs={{0,1},{1,2},{2,3},{3,4},{4,5},{5,6},{6,7},{7,8},{8,9},{9,10},{10,1... | collective-permute-start | bytes 61448 | tf_op jit(solution)/shard_map/ppermute | solution.py:17
  97.7 4.7 collective-permute-start.3
  156.2 15.8 %copy-start.8 = (bf16[256,256]{1,0:T(8,128)(2,1)S(1)}, bf16[256,256]{1,0:T(8,128)(2,1)}, u32[]{:S(2)}) copy-start(bf16[256,256]{1,0:T(8,128)(2,1)} %reshape.386) | copy-start | bytes 393220
  167.5 4.7 copy-start.17
  167.5 4.9 %copy-start.16 = (bf16[256,256]{1,0:T(8,128)(2,1)S(1)}, bf16[256,256]{1,0:T(8,128)(2,1)}, u32[]{:S(2)}) copy-start(bf16[256,256]{1,0:T(8,128)(2,1)} %reshape.388) | copy-start | bytes 393220
  167.5 5.1 %copy-start.11 = (bf16[256,256]{1,0:T(8,128)(2,1)S(1)}, bf16[256,256]{1,0:T(8,128)(2,1)}, u32[]{:S(2)}) copy-start(bf16[256,256]{1,0:T(8,128)(2,1)} %reshape.389) | copy-start | bytes 393220
  167.5 5.3 %copy-start.15 = (bf16[256,256]{1,0:T(8,128)(2,1)S(1)}, bf16[256,256]{1,0:T(8,128)(2,1)}, u32[]{:S(2)}) copy-start(bf16[256,256]{1,0:T(8,128)(2,1)} %reshape.390) | copy-start | bytes 393220
  168.6 4.3 copy-start.14
  169.7 3.4 copy-start.10
  170.9 2.5 copy-start.13
  (21 other events, 24.7 us)
Sparse Core Ops, SparseCore 0:
  185.9 283.2 all-reduce.3
where the time goes:
time: 482 us; the launch traced here: 479 us
  waiting for transfers between devices  294 us (61%)
  local copies, waits for them, and re-layouts  80.7 us (17%)
  starting transfers between devices  57.6 us (12%)
  matrix products  20.7 us (4%)
  between operations  15.1 us (3%)
  other arithmetic  11.4 us (2%)
    psum x1, waiting for transfers between devices, shards(): lax.psum(weight_terms, ('grp', 'blk')) * grad_scale  279 us
    slice x29, local copies, waits for them, and re-layouts, shards(): padded[shift_x:shift_x + size_x, shift_y:shift_y + size_y, shift_z:shift_...  32.4 us
    reshape x26, local copies, waits for them, and re-layouts, shards(): window = padded[shift_x:shift_x + size_x, shift_y:shift_y + size_y, shift...  30.6 us
    all_to_all x1, starting transfers between devices, shards(): lax.all_to_all(send_counts, 'blk', split_axis=0, concat_axis=0, tiled=True)  17.1 us
    ppermute x4, starting transfers between devices, extended(): lax.ppermute(tail, axis, [(i, (i + 1) % count) for i in range(ends)])  14.4 us
    all_to_all x1, starting transfers between devices, shards(): lax.all_to_all(returning, 'blk', split_axis=0, concat_axis=0, tiled=True)  12.7 us
  transfers between devices with their start and end apart: 12, of which 6 were waited for; matrix products, arithmetic and copies ran while one was open for 4% of the time, Pallas kernels for 0%

commit v1 on v0

--- a/solution.py
+++ b/solution.py
@@ -1,9 +1,195 @@
+import functools
 import math
 
 import jax
 import jax.numpy as jnp
 from jax import lax
+from jax.experimental import pallas as pl
+from jax.experimental.pallas import tpu as pltpu
 from jax.sharding import PartitionSpec as P
+
+MESH = pl.DeviceIdType.MESH
+F32, BF16 = jnp.float32, jnp.bfloat16
+SIZES = {"x": 4, "y": 8, "z": 8}
+PARTS = ((0, 11, "xyz"), (11, 8, "yzx"), (19, 8, "zxy"))
+TILE = (8, 128)
+
+
+def part_sizes(part):
+    first, count, axes = part
+    na, nb, nc = (SIZES[a] for a in axes)
+    per_core = count * 32 // 2
+    n_a = per_core // na
+    n_b = -(-n_a // nb)
+    return na, nb, nc, per_core, n_a, n_b
+
+
+def reduce_scratch():
+    shapes = []
+    for part in PARTS:
+        na, nb, nc, per_core, n_a, n_b = part_sizes(part)
+        shapes += [
+            pltpu.VMEM((na, n_a) + TILE, F32),
+            pltpu.VMEM((na - 1, n_a) + TILE, F32),
+            pltpu.VMEM((nb * n_b,) + TILE, F32),
+            pltpu.VMEM((nb - 1, n_b) + TILE, F32),
+            pltpu.VMEM((nc, n_b) + TILE, F32),
+            pltpu.VMEM((nb * n_b,) + TILE, BF16),
+        ]
+        for n in (na, na, nb, nc, nb, na, na):
+            shapes += [pltpu.SemaphoreType.DMA((n,)), pltpu.SemaphoreType.DMA((n,))]
+    return shapes
+
+
+PER_PART = 6 + 14
+
+
+def coords():
+    g, b = lax.axis_index("grp"), lax.axis_index("blk")
+    return {"x": g // 2, "c": g % 2, "y": b // 8, "z": b % 8}
+
+
+def device(at, axis, value):
+    at = dict(at)
+    at[axis] = value
+    return (at["x"] * 2 + at["c"], at["y"] * 8 + at["z"])
+
+
+def greet(at):
+    peers = [device(at, "c", 1 - at["c"])]
+    for axis, n in SIZES.items():
+        peers += [device(at, axis, (at[axis] + r) % n) for r in range(1, n)]
+    return peers
+
+
+def reduce_steps(at, scale, p_ref, out_ref, scratch):
+    c = at["c"]
+    sibling = device(at, "c", 1 - c)
+    plans = []
+    for i, part in enumerate(PARTS):
+        own = scratch[i * PER_PART : (i + 1) * PER_PART]
+        plans.append((part, part_sizes(part), own[:6], own[6:]))
+    sends = []
+
+    def copy(src, dst, send, recv, who):
+        made = pltpu.make_async_remote_copy(
+            src_ref=src, dst_ref=dst, send_sem=send, recv_sem=recv, device_id=who, device_id_type=MESH
+        )
+        made.start()
+        sends.append(made)
+        return made
+
+    def chunk(plan, core, r):
+        (first, _, axes), (na, nb, nc, per_core, n_a, n_b), _, _ = plan
+        return pl.ds(first * 32 + core * per_core + (at[axes[0]] + r) % na * n_a, n_a)
+
+    rounds = [(r, plan) for r in list(range(1, 8)) + [0] for plan in plans if r < plan[1][0]]
+    core_copies = {}
+    for r, plan in rounds:
+        bufs, sems = plan[2], plan[3]
+        core_copies[r, plan[0]] = copy(
+            p_ref.at[chunk(plan, 1 - c, r)], bufs[0].at[r], sems[0].at[r], sems[1].at[r], sibling
+        )
+    a_copies = {}
+    for r, plan in rounds:
+        (first, _, axes), (na, *_), bufs, sems = plan
+        core_copies[r, plan[0]].wait_recv()
+        bufs[0][r] = bufs[0][r] + p_ref[chunk(plan, c, r)]
+        if r:
+            who = device(at, axes[0], (at[axes[0]] + r) % na)
+            a_copies[r, plan[0]] = copy(bufs[0].at[r], bufs[1].at[r - 1], sems[2].at[r], sems[3].at[r], who)
+    yield
+    b_copies = {}
+    for plan in plans:
+        (first, _, axes), (na, nb, nc, per_core, n_a, n_b), bufs, sems = plan
+        total = bufs[0][0]
+        for r in range(1, na):
+            a_copies[r, plan[0]].wait_recv()
+            total = total + bufs[1][r - 1]
+        bufs[2][pl.ds(0, n_a)] = total
+        if n_a < nb * n_b:
+            bufs[2][pl.ds(n_a, nb * n_b - n_a)] = jnp.zeros((nb * n_b - n_a,) + TILE, F32)
+        me = at[axes[1]]
+        for r in range(1, nb):
+            to = (me + r) % nb
+            b_copies[r, plan[0]] = copy(
+                bufs[2].at[pl.ds(to * n_b, n_b)], bufs[3].at[r - 1], sems[4].at[r], sems[5].at[r], device(at, axes[1], to)
+            )
+    yield
+    c_copies = {}
+    for plan in plans:
+        (first, _, axes), (na, nb, nc, per_core, n_a, n_b), bufs, sems = plan
+        total = bufs[2][pl.ds(at[axes[1]] * n_b, n_b)]
+        for r in range(1, nb):
+            b_copies[r, plan[0]].wait_recv()
+            total = total + bufs[3][r - 1]
+        me = at[axes[2]]
+        bufs[4][me] = total
+        for r in range(1, nc):
+            to = (me + r) % nc
+            c_copies[r, plan[0]] = copy(bufs[4].at[me], bufs[4].at[me], sems[6].at[r], sems[7].at[r], device(at, axes[2], to))
+    yield
+    g_copies = {}
+    for plan in plans:
+        (first, _, axes), (na, nb, nc, per_core, n_a, n_b), bufs, sems = plan
+        for r in range(1, nc):
+            c_copies[r, plan[0]].wait_recv()
+        total = bufs[4][0]
+        for i in range(1, nc):
+            total = total + bufs[4][i]
+        me = at[axes[1]]
+        mine = pl.ds(me * n_b, n_b)
+        bufs[5][mine] = (total * scale).astype(BF16)
+        for r in range(1, nb):
+            to = (me + r) % nb
+            g_copies[r, plan[0]] = copy(bufs[5].at[mine], bufs[5].at[mine], sems[8].at[r], sems[9].at[r], device(at, axes[1], to))
+    yield
+    o_copies, f_copies = {}, []
+    for plan in plans:
+        (first, _, axes), (na, nb, nc, per_core, n_a, n_b), bufs, sems = plan
+        for r in range(1, nb):
+            g_copies[r, plan[0]].wait_recv()
+        mine = chunk(plan, c, 0)
+        out_ref[mine] = bufs[5][pl.ds(0, n_a)]
+        whole = bufs[5].at[pl.ds(0, n_a)]
+        for r in range(1, na):
+            to = (at[axes[0]] + r) % na
+            o_copies[r, plan[0]] = copy(whole, out_ref.at[mine], sems[10].at[r], sems[11].at[r], device(at, axes[0], to))
+        f_copies.append(copy(whole, out_ref.at[mine], sems[12].at[0], sems[13].at[0], sibling))
+    for r in range(1, 8):
+        for plan in plans:
+            na, bufs, sems = plan[1][0], plan[2], plan[3]
+            if r < na:
+                o_copies[r, plan[0]].wait_recv()
+                came = out_ref.at[chunk(plan, c, na - r)]
+                f_copies.append(copy(came, came, sems[12].at[r], sems[13].at[r], sibling))
+    yield
+    for made in f_copies:
+        made.wait_recv()
+    for made in sends:
+        made.wait_send()
+
+
+def kernel(scale, p_ref, out_ref, *scratch):
+    at = coords()
+    barrier = pltpu.get_barrier_semaphore()
+    peers = greet(at)
+    for who in peers:
+        pl.semaphore_signal(barrier, inc=1, device_id=who, device_id_type=MESH)
+    pl.semaphore_wait(barrier, len(peers))
+    for _ in reduce_steps(at, scale, p_ref, out_ref, scratch):
+        pass
+
+
+def all_reduce(p, scale):
+    return pl.pallas_call(
+        functools.partial(kernel, scale),
+        out_shape=jax.ShapeDtypeStruct((864, 8, 128), BF16),
+        in_specs=[pl.BlockSpec(memory_space=pltpu.VMEM)],
+        out_specs=pl.BlockSpec(memory_space=pltpu.VMEM),
+        scratch_shapes=reduce_scratch(),
+        compiler_params=pltpu.CompilerParams(collective_id=2, has_side_effects=True, vmem_limit_bytes=40 << 20),
+    )(p)
 
 
 def extended(cells, sides, width):
@@ -34,7 +220,9 @@
     target = dest[:, 0]
     owners = jnp.arange(blk_count, dtype=jnp.int32)
     one_hot = (target[:, None] == owners[None, :]).astype(jnp.int32)
-    slot_rank = jnp.sum((jnp.cumsum(one_hot, axis=0) - one_hot) * one_hot, axis=1)
+    order = jnp.arange(row_count, dtype=jnp.int32)
+    earlier = (target[:, None] == target[None, :]) & (order[None, :] < order[:, None])
+    slot_rank = jnp.sum(earlier.astype(jnp.int32), axis=1)
     send_counts = jnp.sum(one_hot, axis=0).reshape(blk_count, 1)
     slot_index = target * capacity + slot_rank
     outgoing = jnp.zeros((voxel_count, channels), jnp.bfloat16).at[slot_index].set(features)
@@ -100,10 +288,9 @@
             )
         )
     grad_grid = (back_total * occupied).astype(jnp.bfloat16)
-    weight_terms = jnp.stack(partials).reshape(27 * channels, out_channels)
+    weight_terms = jnp.stack(partials).reshape(27 * channels // 8, 8, out_channels)
     grad_scale = 1.0 / math.sqrt(row_count * blk_count * grp_count)
-    weight_grad = (lax.psum(weight_terms, ("grp", "blk")) * grad_scale).astype(jnp.bfloat16)
-    weight_grad = weight_grad.reshape(27, channels, out_channels)
+    weight_grad = all_reduce(weight_terms, grad_scale).reshape(27, channels, out_channels)
     returning = grad_grid[voxel_of_slot].reshape(blk_count, capacity, channels)
     returned = lax.all_to_all(returning, "blk", split_axis=0, concat_axis=0, tiled=True)
     grad_rows = returned.reshape(voxel_count, channels)[slot_index]

time: 482 us -> 255 us (0.53)
  waiting for transfers between devices: 294 us -> 13 us
  Pallas kernels: 0 us -> 53.3 us
  local copies, waits for them, and re-layouts: 80.7 us -> 96.3 us
  between operations: 15.1 us -> 1.96 us
    psum x1 -> x0, waiting for transfers between devices: 279 us -> none  [shards(): lax.psum(weight_terms, ('grp', 'blk')) * grad_scale]
    pallas_call x0 -> x1, Pallas kernels: none -> 53.3 us  [all_reduce(): pl.pallas_call(functools.partial(kernel, scale), out_shape=jax.ShapeDtype...]
    reshape x26, local copies, waits for them, and re-layouts: 30.6 us -> 39.7 us  [shards(): window = padded[shift_x:shift_x + size_x, shift_y:shift_y + size_y, shift...]
    slice x29, local copies, waits for them, and re-layouts: 32.4 us -> 39.8 us  [shards(): padded[shift_x:shift_x + size_x, shift_y:shift_y + size_y, shift_z:shift_...]
  transfers between devices with their start and end apart: 12 -> 11, of which waited for: 6 -> 4; matrix products, arithmetic and copies ran while one was open for 4% -> 8% of each run, Pallas kernels for 0% -> 0%
where the time goes in v1:
time: 255 us; the launch traced here: 253 us
  local copies, waits for them, and re-layouts  96.3 us (38%)
  starting transfers between devices  58.1 us (23%)
  Pallas kernels  53.3 us (21%)
  matrix products  22.1 us (9%)
  waiting for transfers between devices  13 us (5%)
  other arithmetic  7.87 us (3%)
    pallas_call x1, Pallas kernels, all_reduce(): pl.pallas_call(functools.partial(kernel, scale), out_shape=jax.ShapeDtype...  53.3 us
    slice x29, local copies, waits for them, and re-layouts, shards(): padded[shift_x:shift_x + size_x, shift_y:shift_y + size_y, shift_z:shift_...  39.8 us
    reshape x26, local copies, waits for them, and re-layouts, shards(): window = padded[shift_x:shift_x + size_x, shift_y:shift_y + size_y, shift...  39.7 us
    all_to_all x1, starting transfers between devices, shards(): lax.all_to_all(send_counts, 'blk', split_axis=0, concat_axis=0, tiled=True)  17.1 us
    ppermute x4, starting transfers between devices, extended(): lax.ppermute(tail, axis, [(i, (i + 1) % count) for i in range(ends)])  14.5 us
    all_to_all x1, starting transfers between devices, shards(): lax.all_to_all(returning, 'blk', split_axis=0, concat_axis=0, tiled=True)  12.6 us
    dot_general x27, matrix products, shards(): jnp.dot(window, weight[offset], preferred_element_type=jnp.float32)  11 us
    ppermute x4, starting transfers between devices, extended(): lax.ppermute(head, axis, [((i + 1) % count, i) for i in range(ends)])  8.11 us
  transfers between devices with their start and end apart: 11, of which 4 were waited for; matrix products, arithmetic and copies ran while one was open for 8% of the time, Pallas kernels for 0%

profile of v1, /device:TPU:1, one launch (start us, length us, event | category | flops | bytes accessed | tf_op | source)
XLA Modules:
  0.0 252.6 jit_solution(15208953981891354726)
XLA Ops:
  2.1 17.1 %all-to-all-start.1 = ((s32[64,1,1]{2,1,0:T(1,128)}), s32[64,1,1]{2,1,0:T(1,128)S(1)}, u32[]{:S(2)}, u32[]{:S(2)}) async-start(s32[64,1,1]{2,1,0:T(1,128)} %copy.241), calls=%async_computation.1 | async-start | bytes 65536 | tf_op jit(solution)/shard_map/all_to_all | solution.py:237
  23.6 6.4 %all-to-all-done.1 = s32[64,1,1]{2,1,0:T(1,128)S(1)} async-done(((s32[64,1,1]{2,1,0:T(1,128)}), s32[64,1,1]{2,1,0:T(1,128)S(1)}, u32[]{:S(2)}, u32[]{:S(2)}) %all-to-all-start.1) | async-done | bytes 288 | tf_op jit(solution)/shard_map/all_to_all | solution.py:237
  30.0 5.7 %all-to-all-start = ((bf16[64,4,256]{2,1,0:T(4,128)(2,1)}), bf16[64,4,256]{2,1,0:T(4,128)(2,1)S(1)}, u32[]{:S(2)}, u32[]{:S(2)}) async-start(bf16[64,4,256]{2,1,0:T(4,128)(2,1)} %reshape.380), calls=%async_computation | async-start | bytes 262144 | tf_op jit(solution)/shard_map/all_to_all | solution.py:230
  39.7 3.4 %collective-permute-start.5 = (bf16[1,8,4,128]{3,2,1,0:T(4,128)(2,1)S(1)}, bf16[1,8,4,128]{3,2,1,0:T(4,128)(2,1)S(1)}, u32[]{:S(2)}, u32[]{:S(2)}) collective-permute-start(bf16[1,8,4,128]{3,2,1,0:T(4,128)(2,1)S(1)} %bitcast.495), channel_id=1, source_target_pairs={{64,0},{128,64},{192,128},{256,192},{320,256},{384,320},{448,384},... | collective-permute-start | bytes 24584 | tf_op jit(solution)/shard_map/ppermute | solution.py:205
  43.1 3.0 %collective-permute-start.4 = (bf16[1,8,4,128]{3,2,1,0:T(4,128)(2,1)S(1)}, bf16[1,8,4,128]{3,2,1,0:T(4,128)(2,1)S(1)}, u32[]{:S(2)}, u32[]{:S(2)}) collective-permute-start(bf16[1,8,4,128]{3,2,1,0:T(4,128)(2,1)S(1)} %bitcast.494), channel_id=1, source_target_pairs={{0,64},{64,128},{128,192},{192,256},{256,320},{320,384},{384,448},... | collective-permute-start | bytes 24584 | tf_op jit(solution)/shard_map/ppermute | solution.py:203
  47.1 3.2 %collective-permute-start.6 = (bf16[10,1,4,128]{3,2,1,0:T(4,128)(2,1)S(1)}, bf16[10,1,4,128]{3,2,1,0:T(4,128)(2,1)S(1)}, u32[]{:S(2)}, u32[]{:S(2)}) collective-permute-start(bf16[10,1,4,128]{3,2,1,0:T(4,128)(2,1)S(1)} %get-tuple-element.63), channel_id=1, source_target_pairs={{0,1},{1,2},{2,3},{3,4},{4,5},{5,6},{6,7},{7,8},{8,9},{9,10},{10,1... | collective-permute-start | bytes 30728 | tf_op jit(solution)/shard_map/ppermute | solution.py:203
  51.7 3.0 %collective-permute-done.7 = bf16[10,1,4,128]{3,2,1,0:T(4,128)(2,1)S(1)} collective-permute-done((bf16[10,1,4,128]{3,2,1,0:T(4,128)(2,1)S(1)}, bf16[10,1,4,128]{3,2,1,0:T(4,128)(2,1)S(1)}, u32[]{:S(2)}, u32[]{:S(2)}) %collective-permute-start.7) | collective-permute-done | bytes 10272 | tf_op jit(solution)/shard_map/ppermute | solution.py:205
  62.2 5.4 %collective-permute-start = (bf16[1,8,4,256]{3,1,2,0:T(8,128)(2,1)S(1)}, bf16[1,8,4,256]{3,1,2,0:T(8,128)(2,1)S(1)}, u32[]{:S(2)}, u32[]{:S(2)}) collective-permute-start(bf16[1,8,4,256]{3,1,2,0:T(8,128)(2,1)S(1)} %copy.210), channel_id=1, source_target_pairs={{0,64},{64,128},{128,192},{192,256},{256,320},{320,384},{384,448},... | collective-permute-start | bytes 49160 | tf_op jit(solution)/shard_map/ppermute | solution.py:203
  69.7 12.6 %all-to-all-start.2 = ((bf16[64,4,256]{2,1,0:T(4,128)(2,1)}), bf16[64,4,256]{2,1,0:T(4,128)(2,1)S(1)}, u32[]{:S(2)}, u32[]{:S(2)}) async-start(bf16[64,4,256]{2,1,0:T(4,128)(2,1)} %reshape.437), calls=%async_computation.2 | async-start | bytes 262144 | tf_op jit(solution)/shard_map/all_to_all | solution.py:295
  82.4 1.9 collective-permute-start.1
  84.4 3.3 %collective-permute-done.1 = bf16[1,8,4,256]{3,1,2,0:T(8,128)(2,1)S(1)} collective-permute-done((bf16[1,8,4,256]{3,1,2,0:T(8,128)(2,1)S(1)}, bf16[1,8,4,256]{3,1,2,0:T(8,128)(2,1)S(1)}, u32[]{:S(2)}, u32[]{:S(2)}) %collective-permute-start.1) | collective-permute-done | bytes 16416 | tf_op jit(solution)/shard_map/ppermute | solution.py:205
  87.8 2.9 %collective-permute-start.2 = (bf16[10,1,4,256]{3,1,2,0:T(2,128)(2,1)S(1)}, bf16[10,1,4,256]{3,1,2,0:T(2,128)(2,1)S(1)}, u32[]{:S(2)}, u32[]{:S(2)}) collective-permute-start(bf16[10,1,4,256]{3,1,2,0:T(2,128)(2,1)S(1)} %get-tuple-element.48), channel_id=1, source_target_pairs={{0,1},{1,2},{2,3},{3,4},{4,5},{5,6},{6,7},{7,8},{8,9},{9,10},{10,1... | collective-permute-start | bytes 61448 | tf_op jit(solution)/shard_map/ppermute | solution.py:203
  115.5 1.6 copy.232
  118.8 1.6 copy.240
  122.0 1.6 copy.238
  125.2 1.6 copy.237
  128.4 1.6 copy.234
  131.6 1.6 copy.233
  134.8 1.6 copy.231
  138.1 1.6 copy.230
  141.3 1.6 copy.228
  154.2 1.6 copy.223
  157.4 1.6 copy.222
  194.9 53.3 %shard_map.76 = bf16[864,8,128]{2,1,0:T(8,128)(2,1)S(1)} custom-call(f32[864,8,128]{2,1,0:T(8,128)S(1)} %bitcast.464), custom_call_target="tpu_custom_call" | custom-call | tf_op jit(solution)/shard_map/pallas_call | solution.py:185
  (273 shorter events, 111.3 us)
Async XLA Ops:
  2.1 27.9 %all-to-all-start.1 = ((s32[64,1,1]{2,1,0:T(1,128)}), s32[64,1,1]{2,1,0:T(1,128)S(1)}, u32[]{:S(2)}, u32[]{:S(2)}) async-start(s32[64,1,1]{2,1,0:T(1,128)} %copy.241), calls=%async_computation.1 | async-start | bytes 65536 | tf_op jit(solution)/shard_map/all_to_all | solution.py:237
  30.0 30.6 %all-to-all-start = ((bf16[64,4,256]{2,1,0:T(4,128)(2,1)}), bf16[64,4,256]{2,1,0:T(4,128)(2,1)S(1)}, u32[]{:S(2)}, u32[]{:S(2)}) async-start(bf16[64,4,256]{2,1,0:T(4,128)(2,1)} %reshape.380), calls=%async_computation | async-start | bytes 262144 | tf_op jit(solution)/shard_map/all_to_all | solution.py:230
  35.8 19.6 %copy-start.2 = (bf16[27,256,128]{2,1,0:T(8,128)(2,1)S(1)}, bf16[27,256,128]{2,1,0:T(8,128)(2,1)}, u32[]{:S(2)}) copy-start(bf16[27,256,128]{2,1,0:T(8,128)(2,1)} %param.8) | copy-start | bytes 5308420
  39.7 7.4 %collective-permute-start.5 = (bf16[1,8,4,128]{3,2,1,0:T(4,128)(2,1)S(1)}, bf16[1,8,4,128]{3,2,1,0:T(4,128)(2,1)S(1)}, u32[]{:S(2)}, u32[]{:S(2)}) collective-permute-start(bf16[1,8,4,128]{3,2,1,0:T(4,128)(2,1)S(1)} %bitcast.495), channel_id=1, source_target_pairs={{64,0},{128,64},{192,128},{256,192},{320,256},{384,320},{448,384},... | collective-permute-start | bytes 24584 | tf_op jit(solution)/shard_map/ppermute | solution.py:205
  43.1 4.0 %collective-permute-start.4 = (bf16[1,8,4,128]{3,2,1,0:T(4,128)(2,1)S(1)}, bf16[1,8,4,128]{3,2,1,0:T(4,128)(2,1)S(1)}, u32[]{:S(2)}, u32[]{:S(2)}) collective-permute-start(bf16[1,8,4,128]{3,2,1,0:T(4,128)(2,1)S(1)} %bitcast.494), channel_id=1, source_target_pairs={{0,64},{64,128},{128,192},{192,256},{256,320},{320,384},{384,448},... | collective-permute-start | bytes 24584 | tf_op jit(solution)/shard_map/ppermute | solution.py:203
  47.1 11.2 %copy-start.4 = (bf16[8,8,4,128]{3,2,1,0:T(4,128)(2,1)}, bf16[8,8,4,128]{3,2,1,0:T(4,128)(2,1)S(1)}, u32[]{:S(2)}) copy-start(bf16[8,8,4,128]{3,2,1,0:T(4,128)(2,1)S(1)} %multiply_convert_fusion) | copy-start | bytes 196612
  47.1 4.6 %collective-permute-start.6 = (bf16[10,1,4,128]{3,2,1,0:T(4,128)(2,1)S(1)}, bf16[10,1,4,128]{3,2,1,0:T(4,128)(2,1)S(1)}, u32[]{:S(2)}, u32[]{:S(2)}) collective-permute-start(bf16[10,1,4,128]{3,2,1,0:T(4,128)(2,1)S(1)} %get-tuple-element.63), channel_id=1, source_target_pairs={{0,1},{1,2},{2,3},{3,4},{4,5},{5,6},{6,7},{7,8},{8,9},{9,10},{10,1... | collective-permute-start | bytes 30728 | tf_op jit(solution)/shard_map/ppermute | solution.py:203
  50.4 4.4 %collective-permute-start.7 = (bf16[10,1,4,128]{3,2,1,0:T(4,128)(2,1)S(1)}, bf16[10,1,4,128]{3,2,1,0:T(4,128)(2,1)S(1)}, u32[]{:S(2)}, u32[]{:S(2)}) collective-permute-start(bf16[10,1,4,128]{3,2,1,0:T(4,128)(2,1)S(1)} %get-tuple-element.64), channel_id=1, source_target_pairs={{1,0},{2,1},{3,2},{4,3},{5,4},{6,5},{7,6},{8,7},{9,8},{10,9},{11,1... | collective-permute-start | bytes 30728 | tf_op jit(solution)/shard_map/ppermute | solution.py:205
  62.2 30.1 %copy-start.7 = (bf16[256,256]{1,0:T(8,128)(2,1)}, bf16[256,256]{1,0:T(8,128)(2,1)S(1)}, u32[]{:S(2)}) copy-start(bf16[256,256]{1,0:T(8,128)(2,1)S(1)} %scatter_custom_fusion.1) | copy-start | bytes 393220
  62.2 22.1 %collective-permute-start = (bf16[1,8,4,256]{3,1,2,0:T(8,128)(2,1)S(1)}, bf16[1,8,4,256]{3,1,2,0:T(8,128)(2,1)S(1)}, u32[]{:S(2)}, u32[]{:S(2)}) collective-permute-start(bf16[1,8,4,256]{3,1,2,0:T(8,128)(2,1)S(1)} %copy.210), channel_id=1, source_target_pairs={{0,64},{64,128},{128,192},{192,256},{256,320},{320,384},{384,448},... | collective-permute-start | bytes 49160 | tf_op jit(solution)/shard_map/ppermute | solution.py:203
  69.7 24.1 %all-to-all-start.2 = ((bf16[64,4,256]{2,1,0:T(4,128)(2,1)}), bf16[64,4,256]{2,1,0:T(4,128)(2,1)S(1)}, u32[]{:S(2)}, u32[]{:S(2)}) async-start(bf16[64,4,256]{2,1,0:T(4,128)(2,1)} %reshape.437), calls=%async_computation.2 | async-start | bytes 262144 | tf_op jit(solution)/shard_map/all_to_all | solution.py:295
  82.3 9.9 %copy-start.31 = (bf16[8,8,4,256]{3,2,1,0:T(4,128)(2,1)}, bf16[8,8,4,256]{3,2,1,0:T(4,128)(2,1)S(1)}, u32[]{:S(2)}) copy-start(bf16[8,8,4,256]{3,2,1,0:T(4,128)(2,1)S(1)} %reshape.382) | copy-start | bytes 393220
  82.4 5.4 %collective-permute-start.1 = (bf16[1,8,4,256]{3,1,2,0:T(8,128)(2,1)S(1)}, bf16[1,8,4,256]{3,1,2,0:T(8,128)(2,1)S(1)}, u32[]{:S(2)}, u32[]{:S(2)}) collective-permute-start(bf16[1,8,4,256]{3,1,2,0:T(8,128)(2,1)S(1)} %copy.211), channel_id=1, source_target_pairs={{64,0},{128,64},{192,128},{256,192},{320,256},{384,320},{448,384},... | collective-permute-start | bytes 49160 | tf_op jit(solution)/shard_map/ppermute | solution.py:205
  84.4 11.3 %copy-start.46 = (bf16[9,8,4,256]{3,1,2,0:T(8,128)(2,1)}, bf16[9,8,4,256]{3,1,2,0:T(8,128)(2,1)S(1)}, u32[]{:S(2)}) copy-start(bf16[9,8,4,256]{3,1,2,0:T(8,128)(2,1)S(1)} %get-tuple-element.51) | copy-start | bytes 442372
  87.7 8.0 %copy-start.9 = (bf16[10,8,4,256]{3,1,2,0:T(8,128)(2,1)}, bf16[10,8,4,256]{3,1,2,0:T(8,128)(2,1)S(1)}, u32[]{:S(2)}) copy-start(bf16[10,8,4,256]{3,1,2,0:T(8,128)(2,1)S(1)} %get-tuple-element.70) | copy-start | bytes 491524
  87.7 8.0 %copy-start.40 = (bf16[9,8,4,256]{3,1,2,0:T(8,128)(2,1)}, bf16[9,8,4,256]{3,1,2,0:T(8,128)(2,1)S(1)}, u32[]{:S(2)}) copy-start(bf16[9,8,4,256]{3,1,2,0:T(8,128)(2,1)S(1)} %get-tuple-element.69) | copy-start | bytes 442372
  87.8 7.5 %collective-permute-start.2 = (bf16[10,1,4,256]{3,1,2,0:T(2,128)(2,1)S(1)}, bf16[10,1,4,256]{3,1,2,0:T(2,128)(2,1)S(1)}, u32[]{:S(2)}, u32[]{:S(2)}) collective-permute-start(bf16[10,1,4,256]{3,1,2,0:T(2,128)(2,1)S(1)} %get-tuple-element.48), channel_id=1, source_target_pairs={{0,1},{1,2},{2,3},{3,4},{4,5},{5,6},{6,7},{7,8},{8,9},{9,10},{10,1... | collective-permute-start | bytes 61448 | tf_op jit(solution)/shard_map/ppermute | solution.py:203
  90.7 4.7 %collective-permute-start.3 = (bf16[10,1,4,256]{3,1,2,0:T(2,128)(2,1)S(1)}, bf16[10,1,4,256]{3,1,2,0:T(2,128)(2,1)S(1)}, u32[]{:S(2)}, u32[]{:S(2)}) collective-permute-start(bf16[10,1,4,256]{3,1,2,0:T(2,128)(2,1)S(1)} %get-tuple-element.49), channel_id=1, source_target_pairs={{1,0},{2,1},{3,2},{4,3},{5,4},{6,5},{7,6},{8,7},{9,8},{10,9},{11,1... | collective-permute-start | bytes 61448 | tf_op jit(solution)/shard_map/ppermute | solution.py:205
  176.8 7.1 %copy-start.25 = (bf16[256,256]{1,0:T(8,128)(2,1)S(1)}, bf16[256,256]{1,0:T(8,128)(2,1)}, u32[]{:S(2)}) copy-start(bf16[256,256]{1,0:T(8,128)(2,1)} %reshape.390) | copy-start | bytes 393220
  176.8 7.3 %copy-start.29 = (bf16[256,256]{1,0:T(8,128)(2,1)S(1)}, bf16[256,256]{1,0:T(8,128)(2,1)}, u32[]{:S(2)}) copy-start(bf16[256,256]{1,0:T(8,128)(2,1)} %reshape.391) | copy-start | bytes 393220
  194.8 53.4 %copy-start.23 = (bf16[256,256]{1,0:T(8,128)(2,1)S(1)}, bf16[256,256]{1,0:T(8,128)(2,1)}, u32[]{:S(2)}) copy-start(bf16[256,256]{1,0:T(8,128)(2,1)} %reshape.396) | copy-start | bytes 393220
  194.9 53.6 %copy-start.22 = (bf16[256,256]{1,0:T(8,128)(2,1)S(1)}, bf16[256,256]{1,0:T(8,128)(2,1)}, u32[]{:S(2)}) copy-start(bf16[256,256]{1,0:T(8,128)(2,1)} %reshape.397) | copy-start | bytes 393220
  194.9 53.8 %copy-start.15 = (bf16[256,256]{1,0:T(8,128)(2,1)S(1)}, bf16[256,256]{1,0:T(8,128)(2,1)}, u32[]{:S(2)}) copy-start(bf16[256,256]{1,0:T(8,128)(2,1)} %reshape.398) | copy-start | bytes 393220
  194.9 54.0 %copy-start.21 = (bf16[256,256]{1,0:T(8,128)(2,1)S(1)}, bf16[256,256]{1,0:T(8,128)(2,1)}, u32[]{:S(2)}) copy-start(bf16[256,256]{1,0:T(8,128)(2,1)} %reshape.399) | copy-start | bytes 393220
  (35 other events, 66.1 us)

commit v2 on v1

--- a/solution.py
+++ b/solution.py
@@ -53,13 +53,6 @@
     at = dict(at)
     at[axis] = value
     return (at["x"] * 2 + at["c"], at["y"] * 8 + at["z"])
-
-
-def greet(at):
-    peers = [device(at, "c", 1 - at["c"])]
-    for axis, n in SIZES.items():
-        peers += [device(at, axis, (at[axis] + r) % n) for r in range(1, n)]
-    return peers
 
 
 def reduce_steps(at, scale, p_ref, out_ref, scratch):
@@ -170,131 +163,297 @@
         made.wait_send()
 
 
-def kernel(scale, p_ref, out_ref, *scratch):
+VOX, SLOTS, ROWS = 256, 512, 128
+GRP, BLK = 8, 64
+HALO = 160
+BLOCKS = ((0, 4), (4, 4), (8, 4), (12, 4), (16, 1), (17, 1), (18, 1), (19, 1))
+SIDES = ((-1, 0), (1, 0), (0, -1), (0, 1), (-1, -1), (-1, 1), (1, -1), (1, 1))
+
+
+def iota(shape, dim):
+    return lax.broadcasted_iota(jnp.int32, shape, dim)
+
+
+def dot(a, b, dims=((1,), (0,))):
+    return lax.dot_general(a, b, (dims, ((), ())), preferred_element_type=F32)
+
+
+def one(mask):
+    return jnp.where(mask, 1.0, 0.0).astype(BF16)
+
+
+def inner(v):
+    return (v & 3) * 64 + (v >> 5) * 8 + ((v >> 2) & 7)
+
+
+def row_slots(dest_col, by_row):
+    wide = jnp.broadcast_to(dest_col, (ROWS, ROWS))
+    turned = wide.astype(F32).T.astype(jnp.int32)
+    i, j = iota((ROWS, ROWS), 0), iota((ROWS, ROWS), 1)
+    same = wide == turned
+    if by_row:
+        rank = jnp.sum(jnp.where(same & (j < i), 1.0, 0.0), axis=1, keepdims=True)
+        return dest_col * 8 + rank.astype(jnp.int32)
+    rank = jnp.sum(jnp.where(same & (i < j), 1.0, 0.0), axis=0, keepdims=True)
+    return turned[0:1] * 8 + rank.astype(jnp.int32)
+
+
+def spread(shape, slot_dim):
+    slot, half = iota(shape, slot_dim), iota(shape, 1 - slot_dim)
+    return one((half >> 3) * 4 + (half & 3) == slot)
+
+
+def face_source(row):
+    t = row & 31
+    far = jnp.where((row & 32) != 0, 7, 0)
+    x_side = (t >> 3) * 64 + far * 8 + (t & 7)
+    y_side = (t >> 3) * 64 + (t & 7) * 8 + far
+    k = (row - 128) >> 3
+    corner = (row & 3) * 64 + (k >> 1) * 56 + (k & 1) * 7
+    return jnp.where(row < 64, x_side, jnp.where(row < 128, y_side, corner))
+
+
+def cell_source(row, shift_y):
+    z = row // 80
+    x = (row >> 3) - z * 10 - 1
+    y = (row & 7) + (shift_y - 1)
+    in_x, in_y = (x >= 0) & (x < 8), (y >= 0) & (y < 8)
+    right, top = jnp.where(x > 7, 1, 0), jnp.where(y > 7, 1, 0)
+    inside = z * 64 + x * 8 + y
+    x_side = VOX + right * 32 + z * 8 + y
+    y_side = VOX + 64 + top * 32 + z * 8 + x
+    corner = VOX + 128 + right * 16 + top * 8 + z
+    return jnp.where(in_x & in_y, inside, jnp.where(in_y, x_side, jnp.where(in_x, y_side, corner)))
+
+
+def greet_block(barrier, g, b):
+    def signal(r, _):
+        pl.semaphore_signal(barrier, inc=1, device_id=(g, (b + r) % BLK), device_id_type=MESH)
+        return 0
+
+    lax.fori_loop(1, BLK, signal, 0)
+
+
+def start_all_to_all(g, b, out_ref, in_ref, sems):
+    def send(r, _):
+        to = (b + r) % BLK
+        pltpu.make_async_remote_copy(
+            src_ref=out_ref.at[to],
+            dst_ref=in_ref.at[b],
+            send_sem=sems.at[0],
+            recv_sem=sems.at[1],
+            device_id=(g, to),
+            device_id_type=MESH,
+        ).start()
+        return 0
+
+    lax.fori_loop(1, BLK, send, 0)
+
+
+def end_all_to_all(g, b, out_ref, in_ref, sems):
+    pltpu.make_async_remote_copy(
+        src_ref=out_ref.at[pl.ds(0, BLK - 1)],
+        dst_ref=in_ref.at[pl.ds(0, BLK - 1)],
+        send_sem=sems.at[0],
+        recv_sem=sems.at[1],
+        device_id=(g, (b + 1) % BLK),
+        device_id_type=MESH,
+    ).wait()
+
+
+def exchange_kernel(dest_ref, features_ref, place_ref, grad_ref, own_ref, halo_ref, out, came, face, edge, sems, send_sems, recv_sems):
+    g, b = lax.axis_index("grp"), lax.axis_index("blk")
+    barrier = pltpu.get_barrier_semaphore()
+    greet_block(barrier, g, b)
+    for dx in (-1, 1):
+        for dy in (-1, 0, 1):
+            who = ((g + dx + GRP) % GRP, (b + dy + BLK) % BLK)
+            pl.semaphore_signal(barrier, inc=1, device_id=who, device_id_type=MESH)
+
+    slot = row_slots(dest_ref[...], False)
+    half = iota((SLOTS, ROWS), 0)
+    first, second = half == slot, half == slot + 4
+    packed = dot(one(first), features_ref[:, :128]) + dot(one(second), features_ref[:, 128:])
+    held = dot(one(first | second), jnp.ones((ROWS, 128), BF16))
+    out[...] = jnp.where(held > 0.5, packed, jnp.inf).reshape(BLK, 8, 128).astype(BF16)
+    pl.semaphore_wait(barrier, BLK - 1 + 6)
+    start_all_to_all(g, b, out, came, sems)
+    came[b] = out[b]
+
+    places = jnp.broadcast_to(place_ref[...], (8, VOX)).astype(F32).astype(BF16)
+    place8 = dot(places, spread((VOX, SLOTS), 0))[0:1].astype(jnp.int32)
+    hits = iota((VOX, SLOTS), 0) == inner(place8)
+    low = (iota((VOX, SLOTS), 1) & 4) == 0
+    low_hits, high_hits = one(hits & low), one(hits & ~low)
+    order = one(inner(iota((VOX, VOX), 1)) == iota((VOX, VOX), 0))
+    grad = dot(order, grad_ref[...])
+    face_of = one(face_source(iota((HALO, VOX), 0)) == iota((HALO, VOX), 1))
+
+    end_all_to_all(g, b, out, came, sems)
+    got = came[...].astype(F32).reshape(SLOTS, 128)
+    there = got < jnp.inf
+    rows = jnp.where(there, got, 0.0).astype(BF16)
+    left = dot(low_hits, rows).astype(BF16)
+    right = dot(high_hits, rows).astype(BF16)
+    occupied = dot(low_hits, one(there))
+    masked = (grad * occupied).astype(BF16)
+    cells = jnp.concatenate([left, right, masked], axis=1)
+    own_ref[:, 0:384] = cells
+    own_ref[:, 384:512] = occupied.astype(BF16)
+    face[...] = dot(face_of, cells).reshape(HALO // 8, 8, 384).astype(BF16)
+    copies = []
+    for k, ((at, size), (dx, dy)) in enumerate(zip(BLOCKS, SIDES)):
+        back = SIDES.index((-dx, -dy))
+        made = pltpu.make_async_remote_copy(
+            src_ref=face.at[pl.ds(at, size)],
+            dst_ref=edge.at[pl.ds(BLOCKS[back][0], size)],
+            send_sem=send_sems.at[k],
+            recv_sem=recv_sems.at[k],
+            device_id=((g + dx + GRP) % GRP, (b + dy + BLK) % BLK),
+            device_id_type=MESH,
+        )
+        made.start()
+        copies.append(made)
+    row = iota((HALO, 1), 0)
+    k = (row - 128) >> 3
+    on_x = (row < 64) | (row >= 128)
+    on_y = row >= 64
+    x_far = jnp.where(row < 64, row >> 5, k >> 1)
+    y_far = jnp.where(row < 128, (row - 64) >> 5, k & 1)
+    at_x = jnp.where(x_far == 1, jnp.where(g == GRP - 1, 1, 0), jnp.where(g == 0, 1, 0))
+    at_y = jnp.where(y_far == 1, jnp.where(b == BLK - 1, 1, 0), jnp.where(b == 0, 1, 0))
+    beyond_x = on_x & (at_x == 1)
+    beyond_y = on_y & (at_y == 1)
+    beyond = beyond_x | beyond_y
+    for made in copies:
+        made.wait()
+    halo = edge[...].astype(F32).reshape(HALO, 384)
+    halo_ref[...] = jnp.where(beyond, 0.0, halo).astype(BF16)
+
+
+def exchange(dest, features, placement, grad_out):
+    vmem = pl.BlockSpec(memory_space=pltpu.VMEM)
+    return pl.pallas_call(
+        exchange_kernel,
+        out_shape=(jax.ShapeDtypeStruct((VOX, 512), BF16), jax.ShapeDtypeStruct((HALO, 384), BF16)),
+        in_specs=[vmem] * 4,
+        out_specs=(vmem, vmem),
+        scratch_shapes=[
+            pltpu.VMEM((BLK, 8, 128), BF16),
+            pltpu.VMEM((BLK, 8, 128), BF16),
+            pltpu.VMEM((HALO // 8, 8, 384), BF16),
+            pltpu.VMEM((HALO // 8, 8, 384), BF16),
+            pltpu.SemaphoreType.DMA((2,)),
+            pltpu.SemaphoreType.DMA((8,)),
+            pltpu.SemaphoreType.DMA((8,)),
+        ],
+        compiler_params=pltpu.CompilerParams(collective_id=1, has_side_effects=True, vmem_limit_bytes=24 << 20),
+    )(dest, features, placement, grad_out)
+
+
+def convolve_kernel(own_ref, halo_ref, weight_ref, place_ref, terms_ref, output_ref, back_ref, cells_f, cells_g):
+    data = jnp.concatenate([own_ref[:, :384], halo_ref[...]], axis=0)
+    for y in range(3):
+        select = one(cell_source(iota((320, 1), 0), y) == iota((320, VOX + HALO), 1))
+        moved = dot(select, data)
+        for ref, part in ((cells_f, moved[:, :256]), (cells_g, moved[:, 256:])):
+            lanes = part.shape[1]
+            ref[y, 1:5] = part.reshape(4, 10, 8, lanes)
+            ref[y, 0] = jnp.zeros((10, 8, lanes), F32)
+            ref[y, 5] = jnp.zeros((10, 8, lanes), F32)
+    turned = own_ref[:, :256].astype(F32).T.astype(BF16)
+    total = jnp.zeros((VOX, 128), F32)
+    back = jnp.zeros((VOX, 256), F32)
+
+    def window(ref, x, y, z):
+        part = ref[y, z : z + 4, x : x + 8]
+        return part.reshape(VOX, part.shape[-1]).astype(BF16)
+
+    for x in range(3):
+        for y in range(3):
+            k = x * 9 + y * 3
+            seen = jnp.concatenate([window(cells_g, 2 - x, 2 - y, 2 - z) for z in range(3)], axis=1)
+            terms = dot(turned, seen)
+            for z in range(3):
+                terms_ref[(k + z) * 32 : (k + z + 1) * 32] = terms[:, z * 128 : (z + 1) * 128].reshape(32, 8, 128)
+            flat = jnp.concatenate([weight_ref[k + z] for z in range(3)], axis=1)
+            back = back + dot(seen, flat, ((1,), (1,)))
+            near = jnp.concatenate([window(cells_f, x, y, z) for z in range(3)], axis=1)
+            tall = jnp.concatenate([weight_ref[k + z] for z in range(3)], axis=0)
+            total = total + dot(near, tall)
+    occupied = own_ref[:, 384:512].astype(F32)
+    order = one(inner(iota((VOX, VOX), 0)) == iota((VOX, VOX), 1))
+    output_ref[...] = dot(order, (total * occupied).astype(BF16)).astype(BF16)
+    grid_l = (back[:, :128] * occupied).astype(BF16)
+    grid_r = (back[:, 128:] * occupied).astype(BF16)
+    places = jnp.broadcast_to(place_ref[...], (8, VOX)).astype(F32).astype(BF16)
+    place8 = dot(spread((SLOTS, VOX), 1), places, ((1,), (1,)))[:, 0:1].astype(jnp.int32)
+    hits = inner(place8) == iota((SLOTS, VOX), 1)
+    low = (iota((SLOTS, VOX), 0) & 4) == 0
+    sent = dot(one(hits & low), grid_l) + dot(one(hits & ~low), grid_r)
+    back_ref[...] = sent.reshape(BLK, 8, 128).astype(BF16)
+
+
+def convolve(own, halo, weight, placement):
+    vmem = pl.BlockSpec(memory_space=pltpu.VMEM)
+    return pl.pallas_call(
+        convolve_kernel,
+        out_shape=(
+            jax.ShapeDtypeStruct((864, 8, 128), F32),
+            jax.ShapeDtypeStruct((VOX, 128), BF16),
+            jax.ShapeDtypeStruct((BLK, 8, 128), BF16),
+        ),
+        in_specs=[vmem] * 4,
+        out_specs=(vmem,) * 3,
+        scratch_shapes=[pltpu.VMEM((3, 6, 10, 8, 256), F32), pltpu.VMEM((3, 6, 10, 8, 128), F32)],
+        compiler_params=pltpu.CompilerParams(vmem_limit_bytes=40 << 20),
+    )(own, halo, weight, placement)
+
+
+def finish_kernel(scale, terms_ref, back_ref, dest_ref, out_ref, rows_ref, came, sems, *scratch):
+    g, b = lax.axis_index("grp"), lax.axis_index("blk")
     at = coords()
     barrier = pltpu.get_barrier_semaphore()
-    peers = greet(at)
+    greet_block(barrier, g, b)
+    peers = [device(at, "c", 1 - at["c"])] + [device(at, "x", (at["x"] + r) % 4) for r in range(1, 4)]
     for who in peers:
         pl.semaphore_signal(barrier, inc=1, device_id=who, device_id_type=MESH)
-    pl.semaphore_wait(barrier, len(peers))
-    for _ in reduce_steps(at, scale, p_ref, out_ref, scratch):
+    pl.semaphore_wait(barrier, BLK - 1 + len(peers))
+    steps = reduce_steps(at, scale, terms_ref, out_ref, scratch)
+    next(steps)
+    start_all_to_all(g, b, back_ref, came, sems)
+    came[b] = back_ref[b]
+    slot = row_slots(dest_ref[...], True)
+    half = iota((ROWS, SLOTS), 1)
+    low, high = one(half == slot), one(half == slot + 4)
+    next(steps)
+    end_all_to_all(g, b, back_ref, came, sems)
+    rows = came[...].astype(F32).reshape(SLOTS, 128).astype(BF16)
+    rows_ref[:, :128] = dot(low, rows).astype(BF16)
+    rows_ref[:, 128:] = dot(high, rows).astype(BF16)
+    for _ in steps:
         pass
 
 
-def all_reduce(p, scale):
+def finish(terms, back, dest, scale):
+    vmem = pl.BlockSpec(memory_space=pltpu.VMEM)
     return pl.pallas_call(
-        functools.partial(kernel, scale),
-        out_shape=jax.ShapeDtypeStruct((864, 8, 128), BF16),
-        in_specs=[pl.BlockSpec(memory_space=pltpu.VMEM)],
-        out_specs=pl.BlockSpec(memory_space=pltpu.VMEM),
-        scratch_shapes=reduce_scratch(),
+        functools.partial(finish_kernel, scale),
+        out_shape=(jax.ShapeDtypeStruct((864, 8, 128), BF16), jax.ShapeDtypeStruct((ROWS, 256), BF16)),
+        in_specs=[vmem] * 3,
+        out_specs=(vmem, vmem),
+        scratch_shapes=[pltpu.VMEM((BLK, 8, 128), BF16), pltpu.SemaphoreType.DMA((2,))] + reduce_scratch(),
         compiler_params=pltpu.CompilerParams(collective_id=2, has_side_effects=True, vmem_limit_bytes=40 << 20),
-    )(p)
-
-
-def extended(cells, sides, width):
-    for axis, dim in sides:
-        count = lax.axis_size(axis)
-        ends = count - 1
-        head = lax.slice_in_dim(cells, 0, width, axis=dim)
-        tail = lax.slice_in_dim(cells, cells.shape[dim] - width, cells.shape[dim], axis=dim)
-        cells = jnp.concatenate(
-            [
-                lax.ppermute(tail, axis, [(i, (i + 1) % count) for i in range(ends)]),
-                cells,
-                lax.ppermute(head, axis, [((i + 1) % count, i) for i in range(ends)]),
-            ],
-            axis=dim,
-        )
-    return cells
+    )(terms, back, dest)
 
 
 def shards(features, dest, placement, weight, grad_out):
-    row_count, channels = features.shape
-    blk_count = lax.axis_size("blk")
-    grp_count = lax.axis_size("grp")
-    voxel_of_slot = placement[0]
-    voxel_count = voxel_of_slot.shape[0]
-    capacity = voxel_count // blk_count
     size_x, size_y, size_z, out_channels = grad_out.shape
-    target = dest[:, 0]
-    owners = jnp.arange(blk_count, dtype=jnp.int32)
-    one_hot = (target[:, None] == owners[None, :]).astype(jnp.int32)
-    order = jnp.arange(row_count, dtype=jnp.int32)
-    earlier = (target[:, None] == target[None, :]) & (order[None, :] < order[:, None])
-    slot_rank = jnp.sum(earlier.astype(jnp.int32), axis=1)
-    send_counts = jnp.sum(one_hot, axis=0).reshape(blk_count, 1)
-    slot_index = target * capacity + slot_rank
-    outgoing = jnp.zeros((voxel_count, channels), jnp.bfloat16).at[slot_index].set(features)
-    incoming, recv_counts = (
-        lax.all_to_all(
-            outgoing.reshape(blk_count, capacity, channels),
-            "blk",
-            split_axis=0,
-            concat_axis=0,
-            tiled=True,
-        ),
-        lax.all_to_all(send_counts, "blk", split_axis=0, concat_axis=0, tiled=True),
-    )
-    filled = (
-        (jnp.arange(capacity, dtype=jnp.int32)[None, :] < recv_counts)
-        .reshape(-1)
-        .astype(jnp.float32)
-    )
-    voxel_rows = (
-        jnp.zeros((voxel_count, channels), jnp.bfloat16)
-        .at[voxel_of_slot]
-        .set(incoming.reshape(voxel_count, channels))
-    )
-    occupied = jnp.zeros((voxel_count,), jnp.float32).at[voxel_of_slot].set(filled)[:, None]
-    voxel_grid = voxel_rows.reshape(size_x, size_y, size_z, channels)
-    padded = extended(voxel_grid, (("grp", 0), ("blk", 1)), 1)
-    padded = jnp.pad(padded, ((0, 0), (0, 0), (1, 1), (0, 0)))
-    shifted = []
-    total = jnp.zeros((voxel_count, out_channels), jnp.float32)
-    for offset in range(27):
-        shift_x, shift_y, shift_z = (offset // 9, offset // 3 % 3, offset % 3)
-        window = padded[
-            shift_x : shift_x + size_x, shift_y : shift_y + size_y, shift_z : shift_z + size_z
-        ].reshape(voxel_count, channels)
-        shifted.append(window)
-        total = total + jnp.dot(window, weight[offset], preferred_element_type=jnp.float32)
-    output = (total * occupied).astype(jnp.bfloat16).reshape(size_x, size_y, size_z, out_channels)
-    masked_grad = (
-        grad_out.reshape(voxel_count, out_channels).astype(jnp.float32) * occupied
-    ).astype(jnp.bfloat16)
-    grad_padded = extended(
-        masked_grad.reshape(size_x, size_y, size_z, out_channels), (("grp", 0), ("blk", 1)), 1
-    )
-    grad_padded = jnp.pad(grad_padded, ((0, 0), (0, 0), (1, 1), (0, 0)))
-    back_total = jnp.zeros((voxel_count, channels), jnp.float32)
-    partials = []
-    for offset in range(27):
-        shift_x, shift_y, shift_z = (offset // 9, offset // 3 % 3, offset % 3)
-        window = grad_padded[
-            2 - shift_x : 2 - shift_x + size_x,
-            2 - shift_y : 2 - shift_y + size_y,
-            2 - shift_z : 2 - shift_z + size_z,
-        ].reshape(voxel_count, out_channels)
-        back_total = back_total + lax.dot_general(
-            window, weight[offset], (((1,), (1,)), ((), ())), preferred_element_type=jnp.float32
-        )
-        partials.append(
-            lax.dot_general(
-                shifted[offset],
-                masked_grad,
-                (((0,), (0,)), ((), ())),
-                preferred_element_type=jnp.float32,
-            )
-        )
-    grad_grid = (back_total * occupied).astype(jnp.bfloat16)
-    weight_terms = jnp.stack(partials).reshape(27 * channels // 8, 8, out_channels)
-    grad_scale = 1.0 / math.sqrt(row_count * blk_count * grp_count)
-    weight_grad = all_reduce(weight_terms, grad_scale).reshape(27, channels, out_channels)
-    returning = grad_grid[voxel_of_slot].reshape(blk_count, capacity, channels)
-    returned = lax.all_to_all(returning, "blk", split_axis=0, concat_axis=0, tiled=True)
-    grad_rows = returned.reshape(voxel_count, channels)[slot_index]
-    return (output, grad_rows, weight_grad)
+    own, halo = exchange(dest, features, placement, grad_out.reshape(VOX, out_channels))
+    terms, output, back = convolve(own, halo, weight, placement)
+    total = ROWS * lax.axis_size("grp") * lax.axis_size("blk")
+    weight_grad, grad_rows = finish(terms, back, dest, 1.0 / math.sqrt(total))
+    return output.reshape(size_x, size_y, size_z, out_channels), grad_rows, weight_grad.reshape(weight.shape)
 
 
 def solution(mesh):

time: 255 us -> 99.3 us (0.39)
  local copies, waits for them, and re-layouts: 96.3 us -> 7.1 us
  starting transfers between devices: 58.1 us -> 0 us
  Pallas kernels: 53.3 us -> 91.2 us
  matrix products: 22.1 us -> 0 us
  waiting for transfers between devices: 13 us -> 0 us
  other arithmetic: 7.87 us -> 0 us
    reshape x31 -> x0, local copies, waits for them, and re-layouts: 41.2 us -> none  [the longest x26 39.7 us: shards(): window = padded[shift_x:shift_x + size_x, shift_y:shift_y + size_y, shift...]
    slice x38 -> x0, local copies, waits for them, and re-layouts: 40.4 us -> none  [the longest x29 39.8 us: shards(): padded[shift_x:shift_x + size_x, shift_y:shift_y + size_y, shift_z:shift_...]
    pallas_call x1 -> x3, Pallas kernels: 53.3 us -> 91.2 us  [the longest x1 55.5 us: finish(): pl.pallas_call(functools.partial(finish_kernel, scale), out_shape=(jax.Sh...]
    all_to_all x3 -> x0, starting transfers between devices: 35.5 us -> none  [the longest x1 17.1 us: shards(): lax.all_to_all(send_counts, 'blk', split_axis=0, concat_axis=0, tiled=True)]
    ppermute x8 -> x0, starting transfers between devices: 22.6 us -> none  [the longest x4 14.5 us: extended(): lax.ppermute(tail, axis, [(i, (i + 1) % count) for i in range(ends)])]
    dot_general x81 -> x0, matrix products: 22.1 us -> none  [the longest x27 11 us: shards(): jnp.dot(window, weight[offset], preferred_element_type=jnp.float32)]
    ppermute x8 -> x0, waiting for transfers between devices: 6.55 us -> none  [the longest x4 6.54 us: extended(): lax.ppermute(head, axis, [((i + 1) % count, i) for i in range(ends)])]
    all_to_all x3 -> x0, waiting for transfers between devices: 6.44 us -> none  [the longest x1 6.43 us: shards(): lax.all_to_all(send_counts, 'blk', split_axis=0, concat_axis=0, tiled=True)]
  transfers between devices with their start and end apart: 11 -> 0, of which waited for: 4 -> 0; matrix products, arithmetic and copies ran while one was open for 8% -> 0% of each run, Pallas kernels for 0% -> 0%
where the time goes in v2:
time: 99.3 us; the launch traced here: 99 us
  Pallas kernels  91.2 us (92%)
  local copies, waits for them, and re-layouts  7.1 us (7%)
    pallas_call x1, Pallas kernels, finish(): pl.pallas_call(functools.partial(finish_kernel, scale), out_shape=(jax.Sh...  55.5 us
    pallas_call x1, Pallas kernels, exchange(): pl.pallas_call(exchange_kernel, out_shape=(jax.ShapeDtypeStruct((VOX, 512...  31.6 us
    unnamed x13, local copies, waits for them, and re-layouts  7.1 us
    pallas_call x1, Pallas kernels, convolve(): pl.pallas_call(convolve_kernel, out_shape=(jax.ShapeDtypeStruct((864, 8,...  4.12 us

profile of v2, /device:TPU:1, one launch (start us, length us, event | category | flops | bytes accessed | tf_op | source)
XLA Modules:
  0.0 99.0 jit_solution(12597188530399837530)
XLA Ops:
  0.6 0.8 copy.8.dest_ref
  1.4 0.0 copy-start.1
  1.4 0.8 copy-done.1
  2.2 0.0 copy-start.2
  2.2 0.8 copy-done.2
  3.1 0.0 copy-start.3
  3.1 0.7 copy-done.3
  3.8 31.6 %shard_map.76 = (bf16[256,512]{1,0:T(8,128)(2,1)S(1)}, bf16[160,384]{1,0:T(8,128)(2,1)S(1)}) custom-call(s32[128,1]{1,0:T(8,128)S(1)} %copy.8.dest_ref, bf16[128,256]{1,0:T(8,128)(2,1)S(1)} %copy-done.1, s32[1,256]{1,0:T(1,128)S(1)} %copy-done.3, bf16[256,128]{1,0:T(8,128)(2,1)S(1)} %bitcast.4), custom_call_target="tpu_custom_call" | custom-call | tf_op jit(solution)/shard_map/pallas_call | solution.py:336
  35.4 0.0 copy-start
  35.4 1.5 %copy-done = bf16[27,256,128]{2,1,0:T(8,128)(2,1)S(1)} copy-done((bf16[27,256,128]{2,1,0:T(8,128)(2,1)S(1)}, bf16[27,256,128]{2,1,0:T(8,128)(2,1)}, u32[]{:S(2)}) %copy-start) | copy-done | bytes 1769496
  36.9 0.0 copy-start.4
  36.9 0.7 copy-done.4
  37.6 4.1 %shard_map.77 = (f32[864,8,128]{2,1,0:T(8,128)S(1)}, bf16[256,128]{1,0:T(8,128)(2,1)}, bf16[64,8,128]{2,1,0:T(8,128)(2,1)S(1)}) custom-call(bf16[256,512]{1,0:T(8,128)(2,1)S(1)} %get-tuple-element.10.own_ref, bf16[160,384]{1,0:T(8,128)(2,1)S(1)} %get-tuple-element.11.halo_ref, bf16[27,256,128]{2,1,0:T(8,128)(2,1)S(1)} %copy-done, s32[1,256]{1,0:T(1,128)S(1)} %copy-done.4), custom_call_target="tpu_custom_call" | custom-call | tf_op jit(solution)/shard_map/pallas_call | solution.py:399
  41.7 55.5 %shard_map.78 = (bf16[864,8,128]{2,1,0:T(8,128)(2,1)S(1)}, bf16[128,256]{1,0:T(8,128)(2,1)S(1)}) custom-call(f32[864,8,128]{2,1,0:T(8,128)S(1)} %get-tuple-element.13.terms_ref, bf16[64,8,128]{2,1,0:T(8,128)(2,1)S(1)} %get-tuple-element.14.back_ref, s32[128,1]{1,0:T(8,128)S(1)} %copy.8.dest_ref), custom_call_target="tpu_custom_call" | custom-call | tf_op jit(solution)/shard_map/pallas_call | solution.py:440
  97.1 0.6 copy.12
  97.8 1.2 %copy.13 = bf16[27,256,128]{2,1,0:T(8,128)(2,1)} copy(bf16[27,256,128]{2,1,0:T(8,128)(2,1)S(1)} %bitcast.3) | data formatting | bytes 3538944
Async XLA Ops:
  1.4 0.8 copy-start.1
  2.2 0.8 copy-start.2
  3.1 0.7 copy-start.3
  35.4 1.5 %copy-start = (bf16[27,256,128]{2,1,0:T(8,128)(2,1)S(1)}, bf16[27,256,128]{2,1,0:T(8,128)(2,1)}, u32[]{:S(2)}) copy-start(bf16[27,256,128]{2,1,0:T(8,128)(2,1)} %weight_ref.1) | copy-start | bytes 5308420
  36.9 0.7 copy-start.4

commit v3 on v0

v3 whole, which is shorter than its diff:
```python
import math

import jax
import jax.numpy as jnp
from jax import lax
from jax.experimental import pallas as pl
from jax.experimental.pallas import tpu as pltpu
from jax.sharding import PartitionSpec as P

MESH = pl.DeviceIdType.MESH
F32, BF16 = jnp.float32, jnp.bfloat16
SIZES = {"x": 4, "y": 8, "z": 8}
PARTS = ((0, 6, "xyz"), (6, 7, "xzy"), (13, 7, "yzx"), (20, 7, "zyx"))
TILE = (8, 128)


VOX, SLOTS, ROWS = 256, 512, 128
GRP, BLK = 8, 64
HALO = 160
BLOCKS = ((0, 4), (4, 4), (8, 4), (12, 4), (16, 1), (17, 1), (18, 1), (19, 1))
SIDES = ((-1, 0), (1, 0), (0, -1), (0, 1), (-1, -1), (-1, 1), (1, -1), (1, 1))


def iota(shape, dim):
    return lax.broadcasted_iota(jnp.int32, shape, dim)


def dot(a, b, dims=((1,), (0,))):
    return lax.dot_general(a, b, (dims, ((), ())), preferred_element_type=F32)


def one(mask):
    return jnp.where(mask, 1.0, 0.0).astype(BF16)


def inner(v):
    return (v & 3) * 64 + (v >> 5) * 8 + ((v >> 2) & 7)


def part_sizes(part):
    first, count, axes = part
    na, nb, nc = (SIZES[a] for a in axes)
    per_core = count * 32 // 2
    n_a = per_core // na
    n_b = -(-n_a // nb)
    return na, nb, nc, per_core, n_a, n_b


def reduce_scratch():
    shapes = []
    for part in PARTS:
        na, nb, nc, per_core, n_a, n_b = part_sizes(part)
        shapes += [
            pltpu.VMEM((na, n_a) + TILE, F32),
            pltpu.VMEM((na - 1, n_a) + TILE, F32),
            pltpu.VMEM((nb * n_b,) + TILE, F32),
            pltpu.VMEM((nb - 1, n_b) + TILE, F32),
            pltpu.VMEM((nc, n_b) + TILE, F32),
            pltpu.VMEM((nb * n_b,) + TILE, BF16),
        ]
        for n in (na, na, nb, nc, nb, na, na):
            shapes += [pltpu.SemaphoreType.DMA((n,)), pltpu.SemaphoreType.DMA((n,))]
    return shapes


PER_PART = 6 + 14


def coords():
    g, b = lax.axis_index("grp"), lax.axis_index("blk")
    return {"x": g // 2, "c": g % 2, "y": b // 8, "z": b % 8}


def device(at, axis, value):
    at = dict(at)
    at[axis] = value
    return (at["x"] * 2 + at["c"], at["y"] * 8 + at["z"])


def row_slots(dest_row, by_row):
    turned = jnp.broadcast_to(dest_row, (ROWS, ROWS))
    wide = turned.astype(F32).T.astype(jnp.int32)
    i, j = iota((ROWS, ROWS), 0), iota((ROWS, ROWS), 1)
    same = wide == turned
    if by_row:
        rank = jnp.sum(jnp.where(same & (j < i), 1.0, 0.0), axis=1, keepdims=True)
        return wide[:, 0:1] * 8 + rank.astype(jnp.int32)
    rank = jnp.sum(jnp.where(same & (i < j), 1.0, 0.0), axis=0, keepdims=True)
    return dest_row * 8 + rank.astype(jnp.int32)


def spread(shape, slot_dim):
    slot, half = iota(shape, slot_dim), iota(shape, 1 - slot_dim)
    return one((half >> 3) * 4 + (half & 3) == slot)


def face_source(row):
    t = row & 31
    far = jnp.where((row & 32) != 0, 7, 0)
    x_side = (t >> 3) * 64 + far * 8 + (t & 7)
    y_side = (t >> 3) * 64 + (t & 7) * 8 + far
    k = (row - 128) >> 3
    corner = (row & 3) * 64 + (k >> 1) * 56 + (k & 1) * 7
    return jnp.where(row < 64, x_side, jnp.where(row < 128, y_side, corner))


def cell_source(row, shift_y):
    z = row // 80
    x = (row >> 3) - z * 10 - 1
    y = (row & 7) + (shift_y - 1)
    in_x, in_y = (x >= 0) & (x < 8), (y >= 0) & (y < 8)
    right, top = jnp.where(x > 7, 1, 0), jnp.where(y > 7, 1, 0)
    inside = z * 64 + x * 8 + y
    x_side = VOX + right * 32 + z * 8 + y
    y_side = VOX + 64 + top * 32 + z * 8 + x
    corner = VOX + 128 + right * 16 + top * 8 + z
    return jnp.where(in_x & in_y, inside, jnp.where(in_y, x_side, jnp.where(in_x, y_side, corner)))


def greet_block(barrier, g, b):
    def signal(r, _):
        pl.semaphore_signal(barrier, inc=1, device_id=(g, (b + r) % BLK), device_id_type=MESH)
        return 0

    lax.fori_loop(1, BLK, signal, 0)


def start_all_to_all(g, b, out_ref, in_ref, sems):
    def send(r, _):
        to = (b + r) % BLK
        pltpu.make_async_remote_copy(
            src_ref=out_ref.at[to],
            dst_ref=in_ref.at[b],
            send_sem=sems.at[0],
            recv_sem=sems.at[1],
            device_id=(g, to),
            device_id_type=MESH,
        ).start()
        return 0

    lax.fori_loop(1, BLK, send, 0)


def end_all_to_all(g, b, out_ref, in_ref, sems):
    pltpu.make_async_remote_copy(
        src_ref=out_ref.at[pl.ds(0, BLK - 1)],
        dst_ref=in_ref.at[pl.ds(0, BLK - 1)],
        send_sem=sems.at[0],
        recv_sem=sems.at[1],
        device_id=(g, (b + 1) % BLK),
        device_id_type=MESH,
    ).wait()


class Reduction:
    def __init__(self, at, scale, terms, result, scratch):
        self.at, self.scale, self.terms, self.result = at, scale, terms, result
        self.sibling = device(at, "c", 1 - at["c"])
        self.sends, self.flights = [], {}
        self.own = [scratch[i * PER_PART : (i + 1) * PER_PART] for i in range(len(PARTS))]

    def copy(self, key, src, dst, sems, r, who):
        made = pltpu.make_async_remote_copy(
            src_ref=src, dst_ref=dst, send_sem=sems[0].at[r], recv_sem=sems[1].at[r], device_id=who, device_id_type=MESH
        )
        made.start()
        self.sends.append(made)
        self.flights[key] = made

    def took(self, *key):
        self.flights[key].wait_recv()

    def parts(self, i):
        first, _, axes = PARTS[i]
        bufs, sems = self.own[i][:6], self.own[i][6:]
        pairs = [sems[k : k + 2] for k in range(0, 14, 2)]
        return axes, part_sizes(PARTS[i]), bufs, pairs

    def chunk(self, i, core, r):
        first, _, axes = PARTS[i]
        na, _, _, per_core, n_a, _ = part_sizes(PARTS[i])
        return pl.ds(first * 32 + core * per_core + (self.at[axes[0]] + r) % na * n_a, n_a)

    def rounds(self, i):
        na = part_sizes(PARTS[i])[0]
        return [*range(1, na), 0]

    def to_core(self, i):
        axes, _, bufs, pairs = self.parts(i)
        for r in self.rounds(i):
            src = self.terms.at[self.chunk(i, 1 - self.at["c"], r)]
            self.copy(("core", i, r), src, bufs[0].at[r], pairs[0], r, self.sibling)

    def to_first(self, i):
        axes, (na, *_), bufs, pairs = self.parts(i)
        for r in self.rounds(i):
            self.took("core", i, r)
            bufs[0][r] = bufs[0][r] + self.terms[self.chunk(i, self.at["c"], r)]
            if r:
                who = device(self.at, axes[0], (self.at[axes[0]] + r) % na)
                self.copy(("a", i, r), bufs[0].at[r], bufs[1].at[r - 1], pairs[1], r, who)

    def to_second(self, i):
        axes, (na, nb, nc, per_core, n_a, n_b), bufs, pairs = self.parts(i)
        total = bufs[0][0]
        for r in range(1, na):
            self.took("a", i, r)
            total = total + bufs[1][r - 1]
        bufs[2][pl.ds(0, n_a)] = total
        if n_a < nb * n_b:
            bufs[2][pl.ds(n_a, nb * n_b - n_a)] = jnp.zeros((nb * n_b - n_a,) + TILE, F32)
        for r in range(1, nb):
            to = (self.at[axes[1]] + r) % nb
            src = bufs[2].at[pl.ds(to * n_b, n_b)]
            self.copy(("b", i, r), src, bufs[3].at[r - 1], pairs[2], r, device(self.at, axes[1], to))

    def to_third(self, i):
        axes, (na, nb, nc, per_core, n_a, n_b), bufs, pairs = self.parts(i)
        total = bufs[2][pl.ds(self.at[axes[1]] * n_b, n_b)]
        for r in range(1, nb):
            self.took("b", i, r)
            total = total + bufs[3][r - 1]
        me = self.at[axes[2]]
        bufs[4][me] = total
        for r in range(1, nc):
            who = device(self.at, axes[2], (me + r) % nc)
            self.copy(("c", i, r), bufs[4].at[me], bufs[4].at[me], pairs[3], r, who)

    def back_second(self, i):
        axes, (na, nb, nc, per_core, n_a, n_b), bufs, pairs = self.parts(i)
        for r in range(1, nc):
            self.took("c", i, r)
        total = bufs[4][0]
        for k in range(1, nc):
            total = total + bufs[4][k]
        me = self.at[axes[1]]
        mine = pl.ds(me * n_b, n_b)
        bufs[5][mine] = (total * self.scale).astype(BF16)
        for r in range(1, nb):
            who = device(self.at, axes[1], (me + r) % nb)
            self.copy(("d", i, r), bufs[5].at[mine], bufs[5].at[mine], pairs[4], r, who)

    def back_first(self, i):
        axes, (na, nb, nc, per_core, n_a, n_b), bufs, pairs = self.parts(i)
        for r in range(1, nb):
            self.took("d", i, r)
        mine = self.chunk(i, self.at["c"], 0)
        whole = bufs[5].at[pl.ds(0, n_a)]
        for r in range(1, na):
            who = device(self.at, axes[0], (self.at[axes[0]] + r) % na)
            self.copy(("e", i, r), whole, self.result.at[mine], pairs[5], r, who)
        self.copy(("f", i, 0), whole, self.result.at[mine], pairs[6], 0, self.sibling)
        self.result[mine] = bufs[5][pl.ds(0, n_a)]

    def back_core(self, i, r):
        axes, (na, *_), bufs, pairs = self.parts(i)
        self.took("e", i, r)
        came = self.result.at[self.chunk(i, self.at["c"], na - r)]
        self.copy(("f", i, r), came, came, pairs[6], r, self.sibling)

    def end(self):
        for i in range(len(PARTS)):
            for r in self.rounds(i):
                self.took("f", i, r)
        for made in self.sends:
            made.wait_send()


def step_kernel(
    scale,
    dest_hbm,
    features_hbm,
    place_hbm,
    grad_hbm,
    weight_hbm,
    result_ref,
    rows_ref,
    output_ref,
    dest_ref,
    features_ref,
    place_ref,
    grad_ref,
    weight_ref,
    terms_ref,
    out,
    came,
    back_out,
    back_came,
    face,
    edge,
    select_ref,
    cells_f,
    cells_g,
    load_sems,
    sems,
    back_sems,
    send_sems,
    recv_sems,
    *scratch,
):
    g, b = lax.axis_index("grp"), lax.axis_index("blk")
    at = coords()
    pairs = (
        (dest_hbm, dest_ref),
        (features_hbm, features_ref),
        (place_hbm, place_ref),
        (grad_hbm, grad_ref),
        (weight_hbm, weight_ref),
    )
    loads = [pltpu.make_async_copy(src, dst, load_sems.at[k]) for k, (src, dst) in enumerate(pairs)]
    for load in loads:
        load.start()
    barrier = pltpu.get_barrier_semaphore()
    greet_block(barrier, g, b)
    for dx in (-1, 1):
        for dy in (-1, 0, 1):
            who = ((g + dx + GRP) % GRP, (b + dy + BLK) % BLK)
            pl.semaphore_signal(barrier, inc=1, device_id=who, device_id_type=MESH)
    for r in range(1, 4):
        who = device(at, "x", (at["x"] + r) % 4)
        pl.semaphore_signal(barrier, inc=1, device_id=who, device_id_type=MESH)

    loads[0].wait()
    slot = row_slots(dest_ref[...], False)
    half = iota((SLOTS, ROWS), 0)
    first, second = half == slot, half == slot + 4
    loads[1].wait()
    packed = dot(one(first), features_ref[:, :128]) + dot(one(second), features_ref[:, 128:])
    held = dot(one(first | second), jnp.ones((ROWS, 128), BF16))
    out[...] = jnp.where(held > 0.5, packed, jnp.inf).reshape(BLK, 8, 128).astype(BF16)
    pl.semaphore_wait(barrier, BLK - 1 + 6 + 3)
    start_all_to_all(g, b, out, came, sems)
    came[b] = out[b]

    loads[2].wait()
    places = jnp.broadcast_to(place_ref[...], (8, VOX)).astype(F32).astype(BF16)
    place8 = dot(places, spread((VOX, SLOTS), 0))[0:1].astype(jnp.int32)
    hits = iota((VOX, SLOTS), 0) == inner(place8)
    low = (iota((VOX, SLOTS), 1) & 4) == 0
    low_hits, high_hits = one(hits & low), one(hits & ~low)
    loads[3].wait()
    grad = dot(one(inner(iota((VOX, VOX), 1)) == iota((VOX, VOX), 0)), grad_ref[...])
    face_of = one(face_source(iota((HALO, VOX), 0)) == iota((HALO, VOX), 1))
    for y in range(3):
        select_ref[y] = one(cell_source(iota((320, 1), 0), y) == iota((320, VOX + HALO), 1))
    for ref in (cells_f, cells_g):
        for y in range(3):
            for z in (0, 5):
                ref[y, z] = jnp.zeros(ref.shape[2:], F32)
    loads[4].wait()

    end_all_to_all(g, b, out, came, sems)
    got = came[...].astype(F32).reshape(SLOTS, 128)
    there = got < jnp.inf
    rows = jnp.where(there, got, 0.0).astype(BF16)
    left = dot(low_hits, rows).astype(BF16)
    right = dot(high_hits, rows).astype(BF16)
    occupied = dot(low_hits, one(there))
    masked = (grad * occupied).astype(BF16)
    cells = jnp.concatenate([left, right, masked], axis=1)
    face[...] = dot(face_of, cells).reshape(HALO // 8, 8, 384).astype(BF16)
    copies = []
    for k, ((place, size), (dx, dy)) in enumerate(zip(BLOCKS, SIDES)):
        opposite = SIDES.index((-dx, -dy))
        made = pltpu.make_async_remote_copy(
            src_ref=face.at[pl.ds(place, size)],
            dst_ref=edge.at[pl.ds(BLOCKS[opposite][0], size)],
            send_sem=send_sems.at[k],
            recv_sem=recv_sems.at[k],
            device_id=((g + dx + GRP) % GRP, (b + dy + BLK) % BLK),
            device_id_type=MESH,
        )
        made.start()
        copies.append(made)
    row = iota((HALO, 1), 0)
    corner = (row - 128) >> 3
    on_x = (row < 64) | (row >= 128)
    on_y = row >= 64
    x_far = jnp.where(row < 64, row >> 5, corner >> 1)
    y_far = jnp.where(row < 128, (row - 64) >> 5, corner & 1)
    at_x = jnp.where(x_far == 1, jnp.where(g == GRP - 1, 1, 0), jnp.where(g == 0, 1, 0))
    at_y = jnp.where(y_far == 1, jnp.where(b == BLK - 1, 1, 0), jnp.where(b == 0, 1, 0))
    beyond = (on_x & (at_x == 1)) | (on_y & (at_y == 1))
    turned = jnp.concatenate([left, right], axis=1).astype(F32).T.astype(BF16)
    for made in copies:
        made.wait()
    halo = jnp.where(beyond, 0.0, edge[...].astype(F32).reshape(HALO, 384)).astype(BF16)
    data = jnp.concatenate([cells, halo], axis=0)

    def shift(ref, part):
        for y in range(3):
            ref[y, 1:5] = dot(select_ref[y], part).reshape(4, 10, 8, part.shape[1])

    def window(ref, x, y, z):
        part = ref[y, z : z + 4, x : x + 8]
        return part.reshape(VOX, part.shape[-1]).astype(BF16)

    def seen(group):
        x, y = group // 3, group % 3
        return jnp.concatenate([window(cells_g, 2 - x, 2 - y, 2 - z) for z in range(3)], axis=1)

    def near(group):
        x, y = group // 3, group % 3
        return jnp.concatenate([window(cells_f, x, y, z) for z in range(3)], axis=1)

    def contribute(groups):
        for group in groups:
            terms = dot(turned, seen(group))
            for z in range(3):
                k = group * 3 + z
                terms_ref[k * 32 : (k + 1) * 32] = terms[:, z * 128 : (z + 1) * 128].reshape(32, 8, 128)

    shift(cells_g, data[:, 256:])
    summed = Reduction(at, scale, terms_ref, result_ref, scratch)
    contribute((4, 5, 6))
    summed.to_core(2)
    contribute((7, 8))
    summed.to_core(3)
    summed.to_first(2)
    contribute((3, 2))
    summed.to_core(1)
    summed.to_first(3)
    contribute((1, 0))
    summed.to_core(0)
    summed.to_first(1)
    summed.to_first(0)

    shift(cells_f, data[:, :256])
    total = jnp.zeros((VOX, 128), F32)
    back = jnp.zeros((VOX, 256), F32)
    for group in range(9):
        weights = [weight_ref[group * 3 + z] for z in range(3)]
        back = back + dot(seen(group), jnp.concatenate(weights, axis=1), ((1,), (1,)))
        total = total + dot(near(group), jnp.concatenate(weights, axis=0))
    natural = one(inner(iota((VOX, VOX), 0)) == iota((VOX, VOX), 1))
    output_ref[...] = dot(natural, (total * occupied).astype(BF16)).astype(BF16)
    grid_l = (back[:, :128] * occupied).astype(BF16)
    grid_r = (back[:, 128:] * occupied).astype(BF16)
    returned = dot(low_hits, grid_l, ((0,), (0,))) + dot(high_hits, grid_r, ((0,), (0,)))
    back_out[...] = returned.reshape(BLK, 8, 128).astype(BF16)

    order = (0, 1, 2, 3)
    for i in order:
        summed.to_second(i)
    start_all_to_all(g, b, back_out, back_came, back_sems)
    back_came[b] = back_out[b]
    for i in order:
        summed.to_third(i)
    for i in order:
        summed.back_second(i)
    for i in order:
        summed.back_first(i)
    for r in range(1, 8):
        for i in order:
            if r < part_sizes(PARTS[i])[0]:
                summed.back_core(i, r)
    end_all_to_all(g, b, back_out, back_came, back_sems)
    slot = row_slots(dest_ref[...], True)
    half = iota((ROWS, SLOTS), 1)
    rows = back_came[...].astype(F32).reshape(SLOTS, 128).astype(BF16)
    rows_ref[:, :128] = dot(one(half == slot), rows).astype(BF16)
    rows_ref[:, 128:] = dot(one(half == slot + 4), rows).astype(BF16)
    summed.end()


def shards(features, dest, placement, weight, grad_out):
    count = ROWS * lax.axis_size("grp") * lax.axis_size("blk")
    vmem, hbm = pl.BlockSpec(memory_space=pltpu.VMEM), pl.BlockSpec(memory_space=pltpu.HBM)
    tiles = pltpu.VMEM((BLK, 8, 128), BF16)
    weight_grad, grad_rows, output = pl.pallas_call(
        lambda *refs: step_kernel(1.0 / math.sqrt(count), *refs),
        out_shape=(
            jax.ShapeDtypeStruct((864, 8, 128), BF16),
            jax.ShapeDtypeStruct((ROWS, 256), BF16),
            jax.ShapeDtypeStruct((VOX, 128), BF16),
        ),
        in_specs=[hbm] * 5,
        out_specs=(vmem,) * 3,
        scratch_shapes=[
            pltpu.VMEM((1, ROWS), jnp.int32),
            pltpu.VMEM((ROWS, 256), BF16),
            pltpu.VMEM((1, VOX), jnp.int32),
            pltpu.VMEM((VOX, 128), BF16),
            pltpu.VMEM((27, 256, 128), BF16),
            pltpu.VMEM((864, 8, 128), F32),
            tiles,
            tiles,
            tiles,
            tiles,
            pltpu.VMEM((HALO // 8, 8, 384), BF16),
            pltpu.VMEM((HALO // 8, 8, 384), BF16),
            pltpu.VMEM((3, 320, VOX + HALO), BF16),
            pltpu.VMEM((3, 6, 10, 8, 256), F32),
            pltpu.VMEM((3, 6, 10, 8, 128), F32),
            pltpu.SemaphoreType.DMA((5,)),
            pltpu.SemaphoreType.DMA((2,)),
            pltpu.SemaphoreType.DMA((2,)),
            pltpu.SemaphoreType.DMA((8,)),
            pltpu.SemaphoreType.DMA((8,)),
        ]
        + reduce_scratch(),
        name="step",
        compiler_params=pltpu.CompilerParams(collective_id=1, has_side_effects=True, vmem_limit_bytes=48 << 20),
    )(dest.reshape(1, ROWS), features, placement, grad_out.reshape(VOX, 128), weight)
    return output.reshape(grad_out.shape), grad_rows, weight_grad.reshape(weight.shape)


def solution(mesh):
    in_specs = (
        P(("grp", "blk"), None),
        P(("grp", "blk"), None),
        P(("grp", "blk"), None),
        P(),
        P("grp", "blk", None, None),
    )
    out_specs = (P("grp", "blk", None, None), P(("grp", "blk"), None), P())
    return jax.shard_map(shards, mesh=mesh, in_specs=in_specs, out_specs=out_specs, check_vma=False)
```

time: 482 us -> 88.2 us (0.18)
  waiting for transfers between devices: 294 us -> 0 us
  Pallas kernels: 0 us -> 80.4 us
  local copies, waits for them, and re-layouts: 80.7 us -> 6.95 us
  starting transfers between devices: 57.6 us -> 0 us
  matrix products: 20.7 us -> 0 us
  between operations: 15.1 us -> 0.65 us
  other arithmetic: 11.4 us -> 0 us
    psum x1 -> x0, waiting for transfers between devices: 279 us -> none  [shards(): lax.psum(weight_terms, ('grp', 'blk')) * grad_scale]
    pallas_call x0 -> x1, Pallas kernels: none -> 80.4 us  [shards(): pl.pallas_call(lambda *refs: step_kernel(1.0 / math.sqrt(count), *refs),...]
    all_to_all x3 -> x0, starting transfers between devices: 34.7 us -> none  [the longest x1 17.1 us: shards(): lax.all_to_all(send_counts, 'blk', split_axis=0, concat_axis=0, tiled=True)]
    slice x38 -> x0, local copies, waits for them, and re-layouts: 33 us -> none  [the longest x29 32.4 us: shards(): padded[shift_x:shift_x + size_x, shift_y:shift_y + size_y, shift_z:shift_...]
    reshape x31 -> x0, local copies, waits for them, and re-layouts: 32.1 us -> none  [the longest x26 30.6 us: shards(): window = padded[shift_x:shift_x + size_x, shift_y:shift_y + size_y, shift...]
    ppermute x8 -> x0, starting transfers between devices: 22.9 us -> none  [the longest x4 14.4 us: extended(): lax.ppermute(tail, axis, [(i, (i + 1) % count) for i in range(ends)])]
    dot_general x81 -> x0, matrix products: 20.7 us -> none  [the longest x27 8.97 us: shards(): jnp.dot(window, weight[offset], preferred_element_type=jnp.float32)]
    all_to_all x3 -> x0, waiting for transfers between devices: 7.97 us -> none  [the longest x1 7.34 us: shards(): lax.all_to_all(send_counts, 'blk', split_axis=0, concat_axis=0, tiled=True)]
  transfers between devices with their start and end apart: 12 -> 0, of which waited for: 6 -> 0; matrix products, arithmetic and copies ran while one was open for 4% -> 0% of each run, Pallas kernels for 0% -> 0%
where the time goes in v3:
time: 88.2 us; the launch traced here: 88 us
  Pallas kernels  80.4 us (91%)
  local copies, waits for them, and re-layouts  6.95 us (8%)
    pallas_call x1, Pallas kernels, shards(): pl.pallas_call(lambda *refs: step_kernel(1.0 / math.sqrt(count), *refs),...  80.4 us
    unnamed x13, local copies, waits for them, and re-layouts  6.95 us

profile of v3, /device:TPU:1, one launch (start us, length us, event | category | flops | bytes accessed | tf_op | source)
XLA Modules:
  0.0 88.0 jit_solution(16024822885892513106)
XLA Ops:
  0.6 0.0 copy-start
  0.6 1.5 %copy-done = bf16[27,256,128]{2,1,0:T(8,128)(2,1)S(1)} copy-done((bf16[27,256,128]{2,1,0:T(8,128)(2,1)S(1)}, bf16[27,256,128]{2,1,0:T(8,128)(2,1)}, u32[]{:S(2)}) %copy-start) | copy-done | bytes 1769496
  2.1 0.0 copy-start.1
  2.1 0.8 copy-done.1
  2.9 0.0 copy-start.2
  3.0 0.8 copy-done.2
  3.8 0.0 copy-start.3
  3.8 0.7 copy-done.3
  4.5 0.0 copy-start.4
  4.5 0.7 copy-done.4
  5.1 80.4 %step.1 = (bf16[864,8,128]{2,1,0:T(8,128)(2,1)S(1)}, bf16[128,256]{1,0:T(8,128)(2,1)S(1)}, bf16[256,128]{1,0:T(8,128)(2,1)S(1)}) custom-call(s32[1,128]{1,0:T(1,128)S(1)} %bitcast.7, bf16[128,256]{1,0:T(8,128)(2,1)S(1)} %copy-done.1, s32[1,256]{1,0:T(1,128)S(1)} %copy-done.3, bf16[256,128]{1,0:T(8,128)(2,1)S(1)} %bitcast.5, bf16[27,256,128]{2,1,0:T(8,128)(2,1)S(1)} %copy-done), custom_call_target="tpu_custom_call" | custom-call | tf_op jit(solution)/shard_map/step/pallas_call | solution.py:470
  85.5 0.6 copy.11
  86.1 0.6 copy.12
  86.8 1.2 %copy.13 = bf16[27,256,128]{2,1,0:T(8,128)(2,1)} copy(bf16[27,256,128]{2,1,0:T(8,128)(2,1)S(1)} %bitcast.4) | data formatting | bytes 3538944
Async XLA Ops:
  0.6 1.5 %copy-start = (bf16[27,256,128]{2,1,0:T(8,128)(2,1)S(1)}, bf16[27,256,128]{2,1,0:T(8,128)(2,1)}, u32[]{:S(2)}) copy-start(bf16[27,256,128]{2,1,0:T(8,128)(2,1)} %refs_4_.1) | copy-start | bytes 5308420
  2.1 0.8 copy-start.1
  2.9 0.8 copy-start.2
  3.8 0.7 copy-start.3
  4.5 0.7 copy-start.4

commit v4 on v3

--- a/solution.py
+++ b/solution.py
@@ -289,6 +289,7 @@
     face,
     edge,
     select_ref,
+    take_ref,
     cells_f,
     cells_g,
     load_sems,
@@ -343,6 +344,9 @@
     face_of = one(face_source(iota((HALO, VOX), 0)) == iota((HALO, VOX), 1))
     for y in range(3):
         select_ref[y] = one(cell_source(iota((320, 1), 0), y) == iota((320, VOX + HALO), 1))
+    back_slot, half = row_slots(dest_ref[...], True), iota((ROWS, SLOTS), 1)
+    take_ref[0] = one(half == back_slot)
+    take_ref[1] = one(half == back_slot + 4)
     for ref in (cells_f, cells_g):
         for y in range(3):
             for z in (0, 5):
@@ -439,34 +443,56 @@
     returned = dot(low_hits, grid_l, ((0,), (0,))) + dot(high_hits, grid_r, ((0,), (0,)))
     back_out[...] = returned.reshape(BLK, 8, 128).astype(BF16)
 
-    order = (0, 1, 2, 3)
+    order = (1, 2, 3, 0)
     for i in order:
         summed.to_second(i)
+    for i in order:
+        summed.to_third(i)
     start_all_to_all(g, b, back_out, back_came, back_sems)
     back_came[b] = back_out[b]
-    for i in order:
-        summed.to_third(i)
     for i in order:
         summed.back_second(i)
     for i in order:
         summed.back_first(i)
+    end_all_to_all(g, b, back_out, back_came, back_sems)
+    rows = back_came[...].astype(F32).reshape(SLOTS, 128).astype(BF16)
+    rows_ref[:, :128] = dot(take_ref[0], rows).astype(BF16)
+    rows_ref[:, 128:] = dot(take_ref[1], rows).astype(BF16)
     for r in range(1, 8):
         for i in order:
             if r < part_sizes(PARTS[i])[0]:
                 summed.back_core(i, r)
-    end_all_to_all(g, b, back_out, back_came, back_sems)
-    slot = row_slots(dest_ref[...], True)
-    half = iota((ROWS, SLOTS), 1)
-    rows = back_came[...].astype(F32).reshape(SLOTS, 128).astype(BF16)
-    rows_ref[:, :128] = dot(one(half == slot), rows).astype(BF16)
-    rows_ref[:, 128:] = dot(one(half == slot + 4), rows).astype(BF16)
     summed.end()
+
+
+def store_kernel(*refs):
+    count = len(refs) // 2
+    sems = refs[-1]
+    copies = [pltpu.make_async_copy(refs[k], refs[count + k], sems.at[k]) for k in range(count)]
+    for made in copies:
+        made.start()
+    for made in copies:
+        made.wait()
+
+
+def store(arrays):
+    vmem, hbm = pl.BlockSpec(memory_space=pltpu.VMEM), pl.BlockSpec(memory_space=pltpu.HBM)
+    return pl.pallas_call(
+        store_kernel,
+        out_shape=[jax.ShapeDtypeStruct(a.shape, a.dtype) for a in arrays],
+        in_specs=[vmem] * len(arrays),
+        out_specs=[hbm] * len(arrays),
+        scratch_shapes=[pltpu.SemaphoreType.DMA((len(arrays),))],
+        name="store",
+        compiler_params=pltpu.CompilerParams(vmem_limit_bytes=8 << 20),
+    )(*arrays)
 
 
 def shards(features, dest, placement, weight, grad_out):
     count = ROWS * lax.axis_size("grp") * lax.axis_size("blk")
     vmem, hbm = pl.BlockSpec(memory_space=pltpu.VMEM), pl.BlockSpec(memory_space=pltpu.HBM)
     tiles = pltpu.VMEM((BLK, 8, 128), BF16)
+    inputs = (dest.reshape(1, ROWS), features, placement, grad_out.reshape(VOX, 128), weight)
     weight_grad, grad_rows, output = pl.pallas_call(
         lambda *refs: step_kernel(1.0 / math.sqrt(count), *refs),
         out_shape=(
@@ -490,6 +516,7 @@
             pltpu.VMEM((HALO // 8, 8, 384), BF16),
             pltpu.VMEM((HALO // 8, 8, 384), BF16),
             pltpu.VMEM((3, 320, VOX + HALO), BF16),
+            pltpu.VMEM((2, ROWS, SLOTS), BF16),
             pltpu.VMEM((3, 6, 10, 8, 256), F32),
             pltpu.VMEM((3, 6, 10, 8, 128), F32),
             pltpu.SemaphoreType.DMA((5,)),
@@ -500,8 +527,9 @@
         ]
         + reduce_scratch(),
         name="step",
-        compiler_params=pltpu.CompilerParams(collective_id=1, has_side_effects=True, vmem_limit_bytes=48 << 20),
-    )(dest.reshape(1, ROWS), features, placement, grad_out.reshape(VOX, 128), weight)
+        compiler_params=pltpu.CompilerParams(collective_id=1, has_side_effects=True, vmem_limit_bytes=54_000_000),
+    )(*(pltpu.with_memory_space_constraint(a, pltpu.HBM) for a in inputs))
+    weight_grad, grad_rows, output = store((weight_grad, grad_rows, output))
     return output.reshape(grad_out.shape), grad_rows, weight_grad.reshape(weight.shape)
 
 

time: 88.2 us -> 80.4 us (0.912)
  local copies, waits for them, and re-layouts: 6.95 us -> 0 us
    unnamed x13 -> x0, local copies, waits for them, and re-layouts: 6.95 us -> none
    pallas_call x1, Pallas kernels: 80.4 us -> 78.4 us  [shards(): pl.pallas_call(lambda *refs: step_kernel(1.0 / math.sqrt(count), *refs),...]
    pallas_call x0 -> x1, Pallas kernels: none -> 1.26 us  [store(): pl.pallas_call(store_kernel, out_shape=[jax.ShapeDtypeStruct(a.shape, a.d...]
where the time goes in v4:
time: 80.4 us; the launch traced here: 80.3 us
  Pallas kernels  79.7 us (99%)
    pallas_call x1, Pallas kernels, shards(): pl.pallas_call(lambda *refs: step_kernel(1.0 / math.sqrt(count), *refs),...  78.4 us

profile of v4, /device:TPU:1, one launch (start us, length us, event | category | flops | bytes accessed | tf_op | source)
XLA Modules:
  0.0 80.3 jit_solution(1278231329407416215)
XLA Ops:
  0.6 78.4 %step.1 = (bf16[864,8,128]{2,1,0:T(8,128)(2,1)S(1)}, bf16[128,256]{1,0:T(8,128)(2,1)S(1)}, bf16[256,128]{1,0:T(8,128)(2,1)S(1)}) custom-call(s32[1,128]{1,0:T(1,128)} %bitcast.5, bf16[128,256]{1,0:T(8,128)(2,1)} %refs_1_.1, s32[1,256]{1,0:T(1,128)} %refs_2_.1, bf16[256,128]{1,0:T(8,128)(2,1)} %bitcast.4, bf16[27,256,128]{2,1,0:T(8,128)(2,1)} %refs_4_.1), custom_call_target="tpu_custom_call" | custom-call | tf_op jit(solution)/shard_map/step/pallas_call | solution.py:496
  79.0 1.3 %store.1 = (bf16[864,8,128]{2,1,0:T(8,128)(2,1)}, bf16[128,256]{1,0:T(8,128)(2,1)}, bf16[256,128]{1,0:T(8,128)(2,1)}) custom-call(bf16[864,8,128]{2,1,0:T(8,128)(2,1)S(1)} %get-tuple-element.9.refs_0_, bf16[128,256]{1,0:T(8,128)(2,1)S(1)} %get-tuple-element.10.refs_1_, bf16[256,128]{1,0:T(8,128)(2,1)S(1)} %get-tuple-element.11.refs_2_), custom_call_target="tpu_custom_call" | custom-call | tf_op jit(solution)/shard_map/store/pallas_call | solution.py:480

commit v5 on v4

--- a/solution.py
+++ b/solution.py
@@ -125,9 +125,13 @@
     lax.fori_loop(1, BLK, signal, 0)
 
 
+def far_first(i):
+    return 4 + i // 2 - i % 2 * (i // 2 * 2 + 1)
+
+
 def start_all_to_all(g, b, out_ref, in_ref, sems):
-    def send(r, _):
-        to = (b + r) % BLK
+    def send(i, _):
+        to = (b // 8 + far_first(i // 8)) % 8 * 8 + (b % 8 + far_first(i % 8)) % 8
         pltpu.make_async_remote_copy(
             src_ref=out_ref.at[to],
             dst_ref=in_ref.at[b],
@@ -138,7 +142,7 @@
         ).start()
         return 0
 
-    lax.fori_loop(1, BLK, send, 0)
+    lax.fori_loop(0, BLK - 1, send, 0)
 
 
 def end_all_to_all(g, b, out_ref, in_ref, sems):
@@ -152,6 +156,10 @@
     ).wait()
 
 
+def away(n):
+    return sorted(range(1, n), key=lambda r: (-min(r, n - r), r))
+
+
 class Reduction:
     def __init__(self, at, scale, terms, result, scratch):
         self.at, self.scale, self.terms, self.result = at, scale, terms, result
@@ -182,8 +190,7 @@
         return pl.ds(first * 32 + core * per_core + (self.at[axes[0]] + r) % na * n_a, n_a)
 
     def rounds(self, i):
-        na = part_sizes(PARTS[i])[0]
-        return [*range(1, na), 0]
+        return [*away(part_sizes(PARTS[i])[0]), 0]
 
     def to_core(self, i):
         axes, _, bufs, pairs = self.parts(i)
@@ -209,7 +216,7 @@
         bufs[2][pl.ds(0, n_a)] = total
         if n_a < nb * n_b:
             bufs[2][pl.ds(n_a, nb * n_b - n_a)] = jnp.zeros((nb * n_b - n_a,) + TILE, F32)
-        for r in range(1, nb):
+        for r in away(nb):
             to = (self.at[axes[1]] + r) % nb
             src = bufs[2].at[pl.ds(to * n_b, n_b)]
             self.copy(("b", i, r), src, bufs[3].at[r - 1], pairs[2], r, device(self.at, axes[1], to))
@@ -222,7 +229,7 @@
             total = total + bufs[3][r - 1]
         me = self.at[axes[2]]
         bufs[4][me] = total
-        for r in range(1, nc):
+        for r in away(nc):
             who = device(self.at, axes[2], (me + r) % nc)
             self.copy(("c", i, r), bufs[4].at[me], bufs[4].at[me], pairs[3], r, who)
 
@@ -236,7 +243,7 @@
         me = self.at[axes[1]]
         mine = pl.ds(me * n_b, n_b)
         bufs[5][mine] = (total * self.scale).astype(BF16)
-        for r in range(1, nb):
+        for r in away(nb):
             who = device(self.at, axes[1], (me + r) % nb)
             self.copy(("d", i, r), bufs[5].at[mine], bufs[5].at[mine], pairs[4], r, who)
 
@@ -246,7 +253,7 @@
             self.took("d", i, r)
         mine = self.chunk(i, self.at["c"], 0)
         whole = bufs[5].at[pl.ds(0, n_a)]
-        for r in range(1, na):
+        for r in away(na):
             who = device(self.at, axes[0], (self.at[axes[0]] + r) % na)
             self.copy(("e", i, r), whole, self.result.at[mine], pairs[5], r, who)
         self.copy(("f", i, 0), whole, self.result.at[mine], pairs[6], 0, self.sibling)
@@ -326,9 +333,10 @@
     half = iota((SLOTS, ROWS), 0)
     first, second = half == slot, half == slot + 4
     loads[1].wait()
-    packed = dot(one(first), features_ref[:, :128]) + dot(one(second), features_ref[:, 128:])
-    held = dot(one(first | second), jnp.ones((ROWS, 128), BF16))
-    out[...] = jnp.where(held > 0.5, packed, jnp.inf).reshape(BLK, 8, 128).astype(BF16)
+    ones = jnp.ones((ROWS, 128), BF16)
+    packed = dot(one(first), jnp.concatenate([features_ref[:, :128], ones], axis=1))
+    packed = packed + dot(one(second), jnp.concatenate([features_ref[:, 128:], ones], axis=1))
+    out[...] = jnp.where(packed[:, 128:] > 0.5, packed[:, :128], jnp.inf).reshape(BLK, 8, 128).astype(BF16)
     pl.semaphore_wait(barrier, BLK - 1 + 6 + 3)
     start_all_to_all(g, b, out, came, sems)
     came[b] = out[b]
@@ -357,9 +365,9 @@
     got = came[...].astype(F32).reshape(SLOTS, 128)
     there = got < jnp.inf
     rows = jnp.where(there, got, 0.0).astype(BF16)
-    left = dot(low_hits, rows).astype(BF16)
+    both = dot(low_hits, jnp.concatenate([rows, one(there)], axis=1))
+    left, occupied = both[:, :128].astype(BF16), both[:, 128:]
     right = dot(high_hits, rows).astype(BF16)
-    occupied = dot(low_hits, one(there))
     masked = (grad * occupied).astype(BF16)
     cells = jnp.concatenate([left, right, masked], axis=1)
     face[...] = dot(face_of, cells).reshape(HALO // 8, 8, 384).astype(BF16)
@@ -386,14 +394,14 @@
     at_y = jnp.where(y_far == 1, jnp.where(b == BLK - 1, 1, 0), jnp.where(b == 0, 1, 0))
     beyond = (on_x & (at_x == 1)) | (on_y & (at_y == 1))
     turned = jnp.concatenate([left, right], axis=1).astype(F32).T.astype(BF16)
+    for y in range(3):
+        cells_g[y, 1:5] = dot(select_ref[y, :, :VOX], masked).reshape(4, 10, 8, 128)
     for made in copies:
         made.wait()
     halo = jnp.where(beyond, 0.0, edge[...].astype(F32).reshape(HALO, 384)).astype(BF16)
-    data = jnp.concatenate([cells, halo], axis=0)
-
-    def shift(ref, part):
-        for y in range(3):
-            ref[y, 1:5] = dot(select_ref[y], part).reshape(4, 10, 8, part.shape[1])
+    for y in range(3):
+        outer = dot(select_ref[y, :, VOX:], halo[:, 256:]).reshape(4, 10, 8, 128)
+        cells_g[y, 1:5] = cells_g[y, 1:5] + outer
 
     def window(ref, x, y, z):
         part = ref[y, z : z + 4, x : x + 8]
@@ -414,7 +422,6 @@
                 k = group * 3 + z
                 terms_ref[k * 32 : (k + 1) * 32] = terms[:, z * 128 : (z + 1) * 128].reshape(32, 8, 128)
 
-    shift(cells_g, data[:, 256:])
     summed = Reduction(at, scale, terms_ref, result_ref, scratch)
     contribute((4, 5, 6))
     summed.to_core(2)
@@ -429,7 +436,9 @@
     summed.to_first(1)
     summed.to_first(0)
 
-    shift(cells_f, data[:, :256])
+    data = jnp.concatenate([cells[:, :256], halo[:, :256]], axis=0)
+    for y in range(3):
+        cells_f[y, 1:5] = dot(select_ref[y], data).reshape(4, 10, 8, 256)
     total = jnp.zeros((VOX, 128), F32)
     back = jnp.zeros((VOX, 256), F32)
     for group in range(9):

time: 80.4 us -> 75.7 us (0.942)
  Pallas kernels: 79.7 us -> 74.9 us
    pallas_call x1, Pallas kernels: 78.4 us -> 73.6 us  [shards(): pl.pallas_call(lambda *refs: step_kernel(1.0 / math.sqrt(count), *refs),...]
where the time goes in v5:
time: 75.7 us; the launch traced here: 75.6 us
  Pallas kernels  74.9 us (99%)
    pallas_call x1, Pallas kernels, shards(): pl.pallas_call(lambda *refs: step_kernel(1.0 / math.sqrt(count), *refs),...  73.6 us

profile of v5, /device:TPU:1, one launch (start us, length us, event | category | flops | bytes accessed | tf_op | source)
XLA Modules:
  0.0 75.6 jit_solution(6637980556897360314)
XLA Ops:
  0.6 73.6 %step.1 = (bf16[864,8,128]{2,1,0:T(8,128)(2,1)S(1)}, bf16[128,256]{1,0:T(8,128)(2,1)S(1)}, bf16[256,128]{1,0:T(8,128)(2,1)S(1)}) custom-call(s32[1,128]{1,0:T(1,128)} %bitcast.5, bf16[128,256]{1,0:T(8,128)(2,1)} %refs_1_.1, s32[1,256]{1,0:T(1,128)} %refs_2_.1, bf16[256,128]{1,0:T(8,128)(2,1)} %bitcast.4, bf16[27,256,128]{2,1,0:T(8,128)(2,1)} %refs_4_.1), custom_call_target="tpu_custom_call" | custom-call | tf_op jit(solution)/shard_map/step/pallas_call | solution.py:505
  74.3 1.3 %store.1 = (bf16[864,8,128]{2,1,0:T(8,128)(2,1)}, bf16[128,256]{1,0:T(8,128)(2,1)}, bf16[256,128]{1,0:T(8,128)(2,1)}) custom-call(bf16[864,8,128]{2,1,0:T(8,128)(2,1)S(1)} %get-tuple-element.9.refs_0_, bf16[128,256]{1,0:T(8,128)(2,1)S(1)} %get-tuple-element.10.refs_1_, bf16[256,128]{1,0:T(8,128)(2,1)S(1)} %get-tuple-element.11.refs_2_), custom_call_target="tpu_custom_call" | custom-call | tf_op jit(solution)/shard_map/store/pallas_call | solution.py:489

commit v6 on v5

--- a/solution.py
+++ b/solution.py
@@ -452,7 +452,7 @@
     returned = dot(low_hits, grid_l, ((0,), (0,))) + dot(high_hits, grid_r, ((0,), (0,)))
     back_out[...] = returned.reshape(BLK, 8, 128).astype(BF16)
 
-    order = (1, 2, 3, 0)
+    order = (2, 3, 1, 0)
     for i in order:
         summed.to_second(i)
     for i in order:

time: 75.7 us -> 74.3 us (0.982)
  Pallas kernels: 74.9 us -> 73.6 us
    pallas_call x1, Pallas kernels: 73.6 us -> 72.3 us  [shards(): pl.pallas_call(lambda *refs: step_kernel(1.0 / math.sqrt(count), *refs),...]
where the time goes in v6:
time: 74.3 us; the launch traced here: 74.2 us
  Pallas kernels  73.6 us (99%)
    pallas_call x1, Pallas kernels, shards(): pl.pallas_call(lambda *refs: step_kernel(1.0 / math.sqrt(count), *refs),...  72.3 us

profile of v6, /device:TPU:1, one launch (start us, length us, event | category | flops | bytes accessed | tf_op | source)
XLA Modules:
  0.0 74.2 jit_solution(12524177621015477296)
XLA Ops:
  0.6 72.3 %step.1 = (bf16[864,8,128]{2,1,0:T(8,128)(2,1)S(1)}, bf16[128,256]{1,0:T(8,128)(2,1)S(1)}, bf16[256,128]{1,0:T(8,128)(2,1)S(1)}) custom-call(s32[1,128]{1,0:T(1,128)} %bitcast.5, bf16[128,256]{1,0:T(8,128)(2,1)} %refs_1_.1, s32[1,256]{1,0:T(1,128)} %refs_2_.1, bf16[256,128]{1,0:T(8,128)(2,1)} %bitcast.4, bf16[27,256,128]{2,1,0:T(8,128)(2,1)} %refs_4_.1), custom_call_target="tpu_custom_call" | custom-call | tf_op jit(solution)/shard_map/step/pallas_call | solution.py:505
  73.0 1.3 %store.1 = (bf16[864,8,128]{2,1,0:T(8,128)(2,1)}, bf16[128,256]{1,0:T(8,128)(2,1)}, bf16[256,128]{1,0:T(8,128)(2,1)}) custom-call(bf16[864,8,128]{2,1,0:T(8,128)(2,1)S(1)} %get-tuple-element.9.refs_0_, bf16[128,256]{1,0:T(8,128)(2,1)S(1)} %get-tuple-element.10.refs_1_, bf16[256,128]{1,0:T(8,128)(2,1)S(1)} %get-tuple-element.11.refs_2_), custom_call_target="tpu_custom_call" | custom-call | tf_op jit(solution)/shard_map/store/pallas_call | solution.py:489
